TPU v7x, 128 devices: a whole 4x4x4 slice. The times are simulated.
128 devices in a mesh: region: 8 (over z, core), tile: 16 (over y, x).
Axes of the slice: x: 4, y: 4, z: 4, core: 2. Of those that a mesh axis runs over, the one named last changes fastest.
Arguments:
- global_deriv: bfloat16 [24576, 32, 128], P(('region', 'tile')), may hold values from -0.109375 to 0.109375
- local_deriv: bfloat16 [24576, 5, 32], P(('region', 'tile')), may hold values from -4 to 4
- hit_weight: bfloat16 [24576, 32], P(('region', 'tile')), may hold values from 0.25 to 4
- hit_resid: bfloat16 [24576, 32], P(('region', 'tile')), may hold values from -6 to 6
- block_ids: int32 [24576, 32], P(('region', 'tile')), may hold values from 0 to 7
- hit_count: int32 [24576], P(('region', 'tile')), may hold values from 4 to 32
- track_region: int32 [24576, 1], P(('region', 'tile')), may hold values from 0 to 7; in each aligned block of 192 rows (0 to 191, 192 to 383, ...) at most 48 rows name the same one
- block_place: int32 [8], replicated, may hold values from 0 to 7, each once
Outputs:
- normal_matrix: float32 [8, 1024, 1024], P('region', 'tile')
- right_side: float32 [8, 1024], P('region', 'tile')
Inputs may be any that keep to these rules, and one draw needn't show every extreme that they name: `track_region`: among the tracks of one device at most 48 share a region, and in every draw some device has exactly 48 tracks in some region. `block_place`: each position appears once.
All inputs are finite; a program needn't handle non-finite values.
Results may differ from a plain program's by a relative error of at most 0.0029.
Values may be sent and summed in bfloat16 or wider, within the bound.
A program may use at most 128 MiB of HBM per device.

v0:
```python
import jax
import jax.numpy as jnp
from jax import lax
from jax.sharding import PartitionSpec as P


def cholesky_fit(local_slopes, weight, misfit, live_hits):
    masked_w = live_hits * weight
    weighted_l = local_slopes * masked_w[:, None, :]
    gamma_mat = [
        [
            jnp.sum(weighted_l[:, a, :] * local_slopes[:, b, :], axis=1) + (1.0 if a == b else 0.0)
            for b in range(5)
        ]
        for a in range(5)
    ]
    beta_vec = [jnp.sum(weighted_l[:, a, :] * misfit, axis=1) for a in range(5)]
    factor = [[None for b in range(5)] for a in range(5)]
    for j in range(5):
        center = gamma_mat[j][j]
        for k in range(j):
            center = center - factor[j][k] * factor[j][k]
        factor[j][j] = jnp.sqrt(center)
        for i in range(j + 1, 5):
            offdiag = gamma_mat[i][j]
            for k in range(j):
                offdiag = offdiag - factor[i][k] * factor[j][k]
            factor[i][j] = offdiag / factor[j][j]
    solved = []
    solved_rhs = []
    for j in range(5):
        current = weighted_l[:, j, :]
        target = beta_vec[j]
        for k in range(j):
            current = current - factor[j][k][:, None] * solved[k]
            target = target - factor[j][k] * solved_rhs[k]
        solved.append(current / factor[j][j][:, None])
        solved_rhs.append(target / factor[j][j])
    scaled = jnp.stack(solved, axis=1)
    projection = solved[0] * solved_rhs[0][:, None]
    for k in range(1, 5):
        projection = projection + solved[k] * solved_rhs[k][:, None]
    hit_factor = masked_w * misfit - projection
    return (scaled, hit_factor, masked_w)


def fit_tracks(gderiv, packed, block_rows, counts, place):
    hit_slots = block_rows.shape[1]
    blocks = place.shape[0]
    live_hits = (jnp.arange(hit_slots)[None, :] < counts[:, None]).astype(jnp.float32)
    floats = packed.astype(jnp.float32)
    scaled, hit_factor, masked_w = cholesky_fit(
        floats[:, 0:5, :], floats[:, 5, :], floats[:, 6, :], live_hits
    )
    matches = (block_rows[:, :, None] == jnp.arange(blocks)[None, None, :]).astype(jnp.float32)
    placing = (place[:, None] == jnp.arange(blocks)[None, :]).astype(jnp.float32)
    onehot = jnp.einsum("nhb,bp->nhp", matches, placing, precision=lax.Precision.HIGHEST)
    gfloat = gderiv.astype(jnp.float32)
    expanded = scaled[:, :, :, None] * onehot[:, None, :, :]
    spread = jnp.einsum("nchp,nhi->ncpi", expanded, gfloat, precision=lax.Precision.HIGHEST).astype(
        jnp.bfloat16
    )
    weighted = (masked_w[:, :, None] * gfloat).astype(jnp.bfloat16)
    return (spread, weighted, hit_factor.astype(jnp.bfloat16), onehot)


def place_direct(weighted, gderiv, onehot):
    blocks = onehot.shape[2]
    block_size = gderiv.shape[2]
    flat_g = gderiv.reshape(-1, block_size)
    diagonal_part = jnp.zeros((blocks * block_size, blocks * block_size), jnp.float32)
    for column in range(blocks):
        picked = (weighted * onehot[:, :, column, None].astype(jnp.bfloat16)).reshape(
            -1, block_size
        )
        tile_sum = lax.dot_general(
            picked, flat_g, (((0,), (0,)), ((), ())), preferred_element_type=jnp.float32
        )
        diagonal_part = diagonal_part.at[
            column * block_size : (column + 1) * block_size,
            column * block_size : (column + 1) * block_size,
        ].set(tile_sum)
    return diagonal_part


def right_vector(hit_factor, gderiv, onehot):
    block_size = gderiv.shape[2]
    loads = (hit_factor[:, :, None] * onehot.astype(jnp.bfloat16)).reshape(-1, onehot.shape[2])
    summed = lax.dot_general(
        loads,
        gderiv.reshape(-1, block_size),
        (((0,), (0,)), ((), ())),
        preferred_element_type=jnp.float32,
    )
    return summed.reshape(-1)


def local(
    global_deriv,
    local_deriv,
    hit_weight,
    hit_resid,
    block_ids,
    hit_count,
    track_region,
    block_place,
):
    slab_width = block_place.shape[0] * global_deriv.shape[2]
    regions = lax.axis_size("region")
    owning = track_region[:, 0]
    packed = jnp.concatenate([local_deriv, hit_weight[:, None, :], hit_resid[:, None, :]], axis=1)
    spread, weighted, hit_factor, onehot = fit_tracks(
        global_deriv, packed, block_ids, hit_count, block_place
    )

    def region_term(index):
        keeper = (owning == index).astype(jnp.bfloat16)
        flat_spread = (spread * keeper[:, None, None, None]).reshape(-1, slab_width)
        schur = lax.dot_general(
            flat_spread, flat_spread, (((0,), (0,)), ((), ())), preferred_element_type=jnp.float32
        )
        diagonal_part = place_direct(weighted * keeper[:, None, None], global_deriv, onehot)
        return (
            diagonal_part - schur,
            right_vector(hit_factor * keeper[:, None], global_deriv, onehot),
        )

    partials, vectors = lax.map(region_term, jnp.arange(regions))
    matrix_rows, vector_rows = (
        lax.psum_scatter(
            partials.reshape(-1, slab_width), ("region", "tile"), scatter_dimension=0, tiled=True
        ),
        lax.psum_scatter(vectors.reshape(-1), ("region", "tile"), scatter_dimension=0, tiled=True),
    )
    return (matrix_rows.reshape(1, -1, slab_width), vector_rows.reshape(1, -1))


def solution(mesh):
    return jax.shard_map(
        local,
        mesh=mesh,
        in_specs=(
            P(("region", "tile"), None, None),
            P(("region", "tile"), None, None),
            P(("region", "tile"), None),
            P(("region", "tile"), None),
            P(("region", "tile"), None),
            P(("region", "tile")),
            P(("region", "tile"), None),
            P(),
        ),
        out_specs=(P("region", "tile", None), P("region", "tile")),
        check_vma=False,
    )
```

profile of v0, /device:TPU:8, one launch (start us, length us, event | category | flops | bytes accessed | tf_op | source)
XLA Modules:
  0.0 938.0 jit_solution(6951412484969885033)
XLA Ops:
  15.8 2.9 multiply_convert_fusion
  23.7 5.1 fusion.81
  29.4 198.4 %while.24 = (s32[]{:T(128)}, f32[8,1024,1024]{2,1,0:T(8,128)}, f32[8,1024]{1,0:T(8,128)}, s32[8]{0:T(128)}, s32[192]{0:T(256)}, /*index=5*/bf16[192,32,128]{2,0,...) while((s32[]{:T(128)}, f32[8,1024,1024]{2,1,0:T(8,128)}, ...), condition=%wide.region_21.0_spmd, body=%wide.region_20.21_spmd.sunk | while | flops 3651131904 | bytes 53119696 | solution.py:128
  32.0 2.9 fusion.198
  37.9 1.5 fusion.200
  42.6 1.5 fusion.203
  45.7 1.5 fusion.205
  47.5 4.3 bitcast_dynamic-update-slice_fusion.2
  56.8 2.9 fusion.198
  62.7 1.5 fusion.200
  67.3 1.5 fusion.203
  70.4 1.5 fusion.205
  72.2 4.4 bitcast_dynamic-update-slice_fusion.2
  81.6 2.9 fusion.198
  93.7 1.5 fusion.204
  97.0 4.4 bitcast_dynamic-update-slice_fusion.2
  106.4 2.9 fusion.198
  118.5 1.5 fusion.204
  121.9 4.3 bitcast_dynamic-update-slice_fusion.2
  131.2 2.9 fusion.198
  143.3 1.5 fusion.204
  146.7 4.3 bitcast_dynamic-update-slice_fusion.2
  156.0 2.9 fusion.198
  165.0 1.5 fusion.202
  171.4 4.4 bitcast_dynamic-update-slice_fusion.2
  180.8 2.9 fusion.198
  196.2 4.4 bitcast_dynamic-update-slice_fusion.2
  205.6 2.9 fusion.198
  217.7 1.5 fusion.204
  221.1 4.3 bitcast_dynamic-update-slice_fusion.2
  228.5 69.5 %all-reduce.1 = f32[8192]{0:T(1024)S(1)} all-reduce(f32[8192]{0:T(1024)S(1)} %bitcast.317), channel_id=3, replica_groups=mesh['region'=8,'tile'=16] {'region','tile'}, use_global_device_ids=true, to_apply=%region_23.0.clone | all-reduce | flops 8192 | bytes 65536
  298.5 632.6 %reduce-scatter.2.cloned.1.call-done = f32[64,1024]{1,0:T(8,128)} async-done(((f32[8192,1024]{1,0:T(8,128)}), f32[64,1024]{1,0:T(8,128)}) %reduce-scatter.2.cloned.1.call-update) | async-done | bytes 262160 | tf_op jit(solution)/shard_map/reduce_scatter | solution.py:130
  (304 shorter events, 137.4 us)
Async XLA Ops:
  7.2 5.6 copy-start.6
  7.2 5.6 copy-start.20
  7.2 924.0 %reduce-scatter.2.cloned.1.call-start = ((), (), s32[]{:S(2)}) async-start(), calls=%async_computation.1 | async-start | bytes 33816576 | tf_op jit(solution)/shard_map/reduce_scatter | solution.py:130
  8.2 4.8 copy-start.3
  10.9 3.3 copy-start
  13.0 5.6 copy-start.1
  37.9 1.5 copy-start.9
  42.6 1.5 copy-start.12
  47.5 4.3 copy-start.2
  62.7 1.5 copy-start.9
  65.8 1.5 copy-start.11
  67.3 1.5 copy-start.12
  72.2 4.4 copy-start.2
  87.5 1.5 copy-start.9
  92.1 1.5 copy-start.12
  93.7 1.5 copy-start.13
  97.0 4.4 copy-start.2
  112.3 1.5 copy-start.9
  117.0 1.5 copy-start.12
  118.5 1.5 copy-start.13
  121.9 4.4 copy-start.2
  137.1 1.5 copy-start.9
  141.8 1.5 copy-start.12
  143.3 1.5 copy-start.13
  146.7 4.3 copy-start.2
  161.9 1.5 copy-start.9
  165.0 1.5 copy-start.11
  171.4 4.4 copy-start.2
  188.2 1.5 copy-start.10
  196.2 4.4 copy-start.2
  217.7 1.5 copy-start.13
  221.0 4.4 copy-start.2
  (53 other events, 73.4 us)
Sparse Core Ops, SparseCore 0:
  227.9 703.2 reduce-scatter.1
where the time goes:
time: 948 us; the launch traced here: 938 us
  waiting for transfers between devices  633 us (67%)
  matrix products  156 us (16%)
  blocking collectives  69.5 us (7%)
  local copies, waits for them, and re-layouts  42.9 us (5%)
  other arithmetic  21.1 us (2%)
  between operations  14.2 us (1%)
    reduce_scatter x1, waiting for transfers between devices, local(): lax.psum_scatter(partials.reshape(-1, slab_width), ('region', 'tile'), sc...  633 us
    dot_general x64, matrix products, place_direct(): lax.dot_general(picked, flat_g, (((0,), (0,)), ((), ())), preferred_eleme...  109 us
    unnamed x1, blocking collectives  69.5 us
    dot_general x8, matrix products, region_term(): lax.dot_general(flat_spread, flat_spread, (((0,), (0,)), ((), ())), prefe...  34.8 us
  transfers between devices with their start and end apart: 1, of which 1 were waited for; matrix products, arithmetic and copies ran while one was open for 0% of the time, Pallas kernels for 0%

commit v1 on v0

v1 whole, which is shorter than its diff:
```python
import functools

import jax
import jax.numpy as jnp
from jax import lax
from jax.experimental import pallas as pl
from jax.experimental.pallas import tpu as pltpu
from jax.sharding import PartitionSpec as P

BS = 128
BR = 8
HITS = 32
TRK = 192
CAP = 48
N_REGION = 8
HALF = CAP // 2
GROUP = 8
CHUNKS = 16
ROWS = 64
WIDTH = BR * BS
F32 = jnp.float32
BF16 = jnp.bfloat16
DIRS = (
    (1, 0, 0, 1, 0),
    (0, 0, 1, 1, 1),
    (-1, 0, 0, 3, 0),
    (0, 0, -1, 3, 1),
    (0, 1, 0, 2, 0),
    (0, -1, 0, 2, 1),
)


def fit(aux_ref):
    t = jnp.transpose(aux_ref[...].astype(F32))
    slopes = [t[32 * c : 32 * c + 32] for c in range(5)]
    w, r, place = t[160:192], t[192:224], t[224:256]
    wl = [s * w for s in slopes]
    gamma = [[None] * 5 for _ in range(5)]
    for a in range(5):
        for b in range(a + 1):
            gamma[a][b] = jnp.sum(wl[a] * slopes[b], axis=0, keepdims=True) + (1.0 if a == b else 0.0)
    beta = [jnp.sum(wl[a] * r, axis=0, keepdims=True) for a in range(5)]
    factor = [[None] * 5 for _ in range(5)]
    inverse = [None] * 5
    for j in range(5):
        center = gamma[j][j]
        for k in range(j):
            center = center - factor[j][k] * factor[j][k]
        factor[j][j] = jnp.sqrt(center)
        inverse[j] = 1.0 / factor[j][j]
        for i in range(j + 1, 5):
            off = gamma[i][j]
            for k in range(j):
                off = off - factor[i][k] * factor[j][k]
            factor[i][j] = off * inverse[j]
    solved, target = [], []
    for j in range(5):
        cur, tgt = wl[j], beta[j]
        for k in range(j):
            cur = cur - factor[j][k] * solved[k]
            tgt = tgt - factor[j][k] * target[k]
        solved.append(cur * inverse[j])
        target.append(tgt * inverse[j])
    hit = w * r
    for k in range(5):
        hit = hit - solved[k] * target[k]
    full = jnp.concatenate(solved + [hit, w, place], axis=0)
    return jnp.transpose(full).astype(BF16)


def kernel(
    idx_ref, g_ref, aux_ref, slot_ref,
    out_ref, vec_ref,
    gsend, grecv, asend, arecv, fitted, lhs, s_buf, d_acc, v_acc, psend, precv, vrecv,
    gs_sem, gr_sem, as_sem, ar_sem, ps_sem, pr_sem, vs_sem, vr_sem,
):
    region = lax.axis_index("region")
    tile = lax.axis_index("tile")
    z, core = region // 2, region % 2
    y, x = tile // 4, tile % 4
    colour = (x + 2 * y + z) % 4

    def device(nx, ny, nz, ncore):
        return {"region": nz * 2 + ncore, "tile": ny * 4 + nx}

    def neighbour(d, ncore):
        dx, dy, dz = DIRS[d][:3]
        return device((x + dx + 4) % 4, (y + dy + 4) % 4, (z + dz + 4) % 4, ncore)

    sibling = device(x, y, z, 1 - core)

    barrier = pltpu.get_barrier_semaphore()
    for d in range(6):
        for c in range(2):
            pl.semaphore_signal(barrier, inc=1, device_id=neighbour(d, c))
    pl.semaphore_signal(barrier, inc=1, device_id=sibling)

    def worker_of(i, rz):
        wy, wx = i // 4, i % 4
        return {"region": ((rz - wx - 2 * wy + 12) % 4) * 2 + core, "tile": i}

    own_worker = (x + 2 * y) % 4 == 0

    def greet(i, carry):
        @pl.when(jnp.logical_not(jnp.logical_and(own_worker, i == tile)))
        def _():
            pl.semaphore_signal(barrier, inc=1, device_id=worker_of(i, z))
        return carry

    lax.fori_loop(0, 16, greet, 0)
    pl.semaphore_wait(barrier, jnp.where(own_worker, 28, 29))

    def gather(q, ref, k):
        def body(i, carry):
            ref[k, i] = g_ref[idx_ref[q * HALF + i]]
            return carry
        lax.fori_loop(0, HALF, body, 0, unroll=4)

    def chunk_of(d, c):
        step, half = DIRS[d][3:]
        return (((colour + step) % 4) * 2 + c) * 2 + half

    def g_copy(d, c):
        k = d * 2 + c
        return pltpu.make_async_remote_copy(
            src_ref=gsend.at[k], dst_ref=grecv.at[d * 2 + core],
            send_sem=gs_sem.at[k], recv_sem=gr_sem.at[d * 2 + core],
            device_id=neighbour(d, c))

    def a_copy(d, c):
        k = d * 2 + c
        return pltpu.make_async_remote_copy(
            src_ref=asend.at[k], dst_ref=arecv.at[d * 2 + core],
            send_sem=as_sem.at[k], recv_sem=ar_sem.at[d * 2 + core],
            device_id=neighbour(d, c))

    def g_sib(h):
        return pltpu.make_async_remote_copy(
            src_ref=gsend.at[12 + h], dst_ref=grecv.at[12 + 2 * core + h],
            send_sem=gs_sem.at[12 + h], recv_sem=gr_sem.at[12 + 2 * core + h],
            device_id=sibling)

    def a_sib(h):
        return pltpu.make_async_remote_copy(
            src_ref=asend.at[12 + h], dst_ref=arecv.at[12 + 2 * core + h],
            send_sem=as_sem.at[12 + h], recv_sem=ar_sem.at[12 + 2 * core + h],
            device_id=sibling)

    for d in range(6):
        for c in range(2):
            gather(chunk_of(d, c), gsend, d * 2 + c)
            g_copy(d, c).start()
    for h in range(2):
        gather((colour * 2 + 1 - core) * 2 + h, gsend, 12 + h)
        g_sib(h).start()
    for h in range(2):
        gather((colour * 2 + core) * 2 + h, grecv, 12 + 2 * core + h)

    fitted[...] = fit(aux_ref)
    slot = slot_ref[...]

    def pick(q):
        rows = q * HALF + lax.broadcasted_iota(jnp.int32, (HALF, 256), 0)
        onehot = jnp.where(slot == rows, 1.0, 0.0).astype(BF16)
        return jnp.dot(onehot, fitted[...], preferred_element_type=F32).astype(BF16)

    for d in range(6):
        for c in range(2):
            asend[d * 2 + c] = pick(chunk_of(d, c))
            a_copy(d, c).start()
    for h in range(2):
        asend[12 + h] = pick((colour * 2 + 1 - core) * 2 + h)
        a_sib(h).start()
    for h in range(2):
        arecv[12 + 2 * core + h] = pick((colour * 2 + core) * 2 + h)

    d_acc[...] = jnp.zeros_like(d_acc)
    v_acc[...] = jnp.zeros_like(v_acc)

    lane = lax.broadcasted_iota(jnp.int32, (GROUP, 128), 1)
    track = lax.broadcasted_iota(jnp.int32, (GROUP, 128), 0)
    residue = track % 4
    blocks = [(lane // HITS + 4 * v) == track for v in range(2)]
    subf = lax.broadcasted_iota(jnp.int32, (GROUP, 256), 0).astype(F32)

    def chunk(m, carry):
        n = jnp.where(m < 2, 12 + 2 * core + m, jnp.where(m < 4, 12 + 2 * (1 - core) + m - 2, m - 4))

        @pl.when(m >= 2)
        def _():
            pltpu.make_async_remote_copy(
                src_ref=gsend.at[0], dst_ref=grecv.at[n], send_sem=gs_sem.at[0],
                recv_sem=gr_sem.at[n], device_id=sibling).wait_recv()
            pltpu.make_async_remote_copy(
                src_ref=asend.at[0], dst_ref=arecv.at[n], send_sem=as_sem.at[0],
                recv_sem=ar_sem.at[n], device_id=sibling).wait_recv()

        a = arecv[n].astype(F32)
        g = grecv[n].reshape(HALF * HITS, BS)
        gt = jnp.transpose(g)
        parts, wps = [], []
        vec = None
        for j in range(3):
            aj = a[GROUP * j : GROUP * j + GROUP]

            turned = []
            for v in range(2):
                half = aj[:, 128 * v : 128 * v + 128]
                turned.append([half] + [pltpu.roll(half, HITS * k, 1) for k in range(1, 4)])

            def spread_lanes(q):
                options = turned[q // 4]
                own_turn = options[(3 - q) % 4]
                for k in range(3):
                    own_turn = jnp.where(residue == k, options[(k - q) % 4], own_turn)
                return jnp.concatenate([jnp.where(b, own_turn, 0.0) for b in blocks], axis=1)

            place = spread_lanes(7)
            base = [spread_lanes(q) for q in range(5)]
            rows = []
            for p in range(BR):
                here = place == float(p)
                rows.extend(jnp.where(here, b, 0.0) for b in base)
            left = jnp.concatenate(rows, axis=0).astype(BF16)
            gj = g[256 * j : 256 * j + 256]
            parts.append(jnp.dot(left, gj, preferred_element_type=F32))
            prow = jnp.sum(place, axis=0, keepdims=True)
            hrow = jnp.sum(spread_lanes(5), axis=0, keepdims=True)
            wrow = jnp.sum(spread_lanes(6), axis=0, keepdims=True)
            onp = subf == prow
            vj = jnp.dot(jnp.where(onp, hrow, 0.0).astype(BF16), gj, preferred_element_type=F32)
            vec = vj if vec is None else vec + vj
            wps.append(jnp.where(onp, wrow, 0.0).astype(BF16))
        v_acc[...] += vec
        wp = jnp.concatenate(wps, axis=1)
        pad = jnp.zeros((8, BS), F32)
        for p in range(BR):
            piece = jnp.concatenate([q[40 * p : 40 * p + 40] for q in parts] + [pad], axis=0)
            s_buf[pl.ds(pl.multiple_of(m * 128, 128), 128), BS * p : BS * p + BS] = piece.astype(BF16)
            lhs[BS * p : BS * p + BS, :] = gt * wp[p : p + 1, :]
        d_acc[...] += jnp.dot(lhs[...], g, preferred_element_type=F32)
        return carry

    lax.fori_loop(0, CHUNKS, chunk, 0)

    def p_copy(i):
        return pltpu.make_async_remote_copy(
            src_ref=psend.at[i], dst_ref=precv.at[tile],
            send_sem=ps_sem.at[i], recv_sem=pr_sem.at[tile],
            device_id={"region": colour * 2 + core, "tile": i})

    def v_copy(i):
        return pltpu.make_async_remote_copy(
            src_ref=v_acc, dst_ref=vrecv.at[tile],
            send_sem=vs_sem.at[i], recv_sem=vr_sem.at[tile],
            device_id={"region": colour * 2 + core, "tile": i})

    def is_self(i):
        return jnp.logical_and(own_worker, i == tile)

    def piece(a, carry):
        cols = pl.ds(pl.multiple_of(a * 256, 256), 256)
        prod = lax.dot_general(
            s_buf[:, cols], s_buf[...], (((0,), (0,)), ((), ())), preferred_element_type=F32)
        lhs_cols = lax.broadcasted_iota(jnp.int32, (1, WIDTH), 1) // BS
        for e in range(2):
            dblock = d_acc[pl.ds(pl.multiple_of(a * 256 + e * 128, 128), 128), :]
            wide = jnp.concatenate([dblock] * BR, axis=1)
            part = jnp.where(lhs_cols == a * 2 + e, wide, 0.0) - prod[e * 128 : e * 128 + 128]
            part = part.astype(BF16)
            for u in range(2):
                psend[a * 4 + e * 2 + u] = part[ROWS * u : ROWS * u + ROWS]
        for u in range(4):
            i = a * 4 + u

            @pl.when(jnp.logical_not(is_self(i)))
            def _():
                p_copy(i).start()
                v_copy(i).start()

            @pl.when(is_self(i))
            def _():
                precv[tile] = psend[i]
                vrecv[tile] = v_acc[...]
        return carry

    lax.fori_loop(0, 4, piece, 0)

    def collect(i, carry):
        @pl.when(jnp.logical_not(is_self(i)))
        def _():
            pltpu.make_async_remote_copy(
                src_ref=psend.at[0], dst_ref=precv.at[i], send_sem=ps_sem.at[0],
                recv_sem=pr_sem.at[i], device_id=sibling).wait_recv()
            pltpu.make_async_remote_copy(
                src_ref=v_acc, dst_ref=vrecv.at[i], send_sem=vs_sem.at[0],
                recv_sem=vr_sem.at[i], device_id=sibling).wait_recv()
        return carry

    lax.fori_loop(0, 16, collect, 0)

    total = precv[0].astype(F32)
    vtot = vrecv[0]
    for i in range(1, 16):
        total = total + precv[i].astype(F32)
        vtot = vtot + vrecv[i]
    out_ref[0] = total
    mine = lax.broadcasted_iota(jnp.int32, (BR, BS), 0) == tile // 2
    row = jnp.sum(jnp.where(mine, vtot, 0.0), axis=0, keepdims=True)
    vec_ref[...] = jnp.where(tile % 2 == 0, row[:, :ROWS], row[:, ROWS:])

    for d in range(6):
        for c in range(2):
            g_copy(d, c).wait_send()
            a_copy(d, c).wait_send()
    for h in range(2):
        g_sib(h).wait_send()
        a_sib(h).wait_send()

    def finish(i, carry):
        @pl.when(jnp.logical_not(is_self(i)))
        def _():
            p_copy(i).wait_send()
            v_copy(i).wait_send()
        return carry

    lax.fori_loop(0, 16, finish, 0)


def local(
    global_deriv,
    local_deriv,
    hit_weight,
    hit_resid,
    block_ids,
    hit_count,
    track_region,
    block_place,
):
    own = track_region[:, 0]
    order = jnp.arange(TRK)
    before = (own[:, None] == own[None, :]) & (order[None, :] < order[:, None])
    slot = own * CAP + jnp.sum(before.astype(jnp.int32), axis=1)
    slots = jnp.arange(N_REGION * CAP)
    index = jnp.sum(jnp.where(slot[None, :] == slots[:, None], order[None, :], 0), axis=1).astype(jnp.int32)
    live = jnp.arange(HITS)[None, :] < hit_count[:, None]
    weight = jnp.where(live, hit_weight, jnp.zeros_like(hit_weight))
    place = jnp.zeros(block_ids.shape, jnp.int32)
    for b in range(BR):
        place = place + jnp.where(block_ids == b, block_place[b], 0)
    aux = jnp.concatenate(
        [local_deriv.reshape(TRK, 5 * HITS), weight, hit_resid, place.astype(BF16)], axis=1)
    aux = jnp.pad(aux, ((0, 256 - TRK), (0, 0)))
    slot_row = jnp.pad(slot.astype(jnp.int32), (0, 256 - TRK), constant_values=-1)[None, :]
    vmem = pl.BlockSpec(memory_space=pltpu.VMEM)
    dma = pltpu.SemaphoreType.DMA
    return pl.pallas_call(
        kernel,
        name="assemble",
        out_shape=(
            jax.ShapeDtypeStruct((1, ROWS, WIDTH), F32),
            jax.ShapeDtypeStruct((1, ROWS), F32),
        ),
        in_specs=[pl.BlockSpec(memory_space=pltpu.SMEM), vmem, vmem, vmem],
        out_specs=(vmem, vmem),
        scratch_shapes=[
            pltpu.VMEM((14, HALF, HITS, BS), BF16),
            pltpu.VMEM((CHUNKS, HALF, HITS, BS), BF16),
            pltpu.VMEM((14, HALF, 256), BF16),
            pltpu.VMEM((CHUNKS, HALF, 256), BF16),
            pltpu.VMEM((256, 256), BF16),
            pltpu.VMEM((WIDTH, HALF * HITS), BF16),
            pltpu.VMEM((CHUNKS * 128, WIDTH), BF16),
            pltpu.VMEM((WIDTH, BS), F32),
            pltpu.VMEM((BR, BS), F32),
            pltpu.VMEM((16, ROWS, WIDTH), BF16),
            pltpu.VMEM((16, ROWS, WIDTH), BF16),
            pltpu.VMEM((16, BR, BS), F32),
            dma((14,)), dma((16,)), dma((14,)), dma((16,)),
            dma((16,)), dma((16,)), dma((16,)), dma((16,)),
        ],
        compiler_params=pltpu.CompilerParams(
            collective_id=0, has_side_effects=True, vmem_limit_bytes=56 << 20),
    )(index, global_deriv, aux, slot_row)


def solution(mesh):
    return jax.shard_map(
        local,
        mesh=mesh,
        in_specs=(
            P(("region", "tile"), None, None),
            P(("region", "tile"), None, None),
            P(("region", "tile"), None),
            P(("region", "tile"), None),
            P(("region", "tile"), None),
            P(("region", "tile")),
            P(("region", "tile"), None),
            P(),
        ),
        out_specs=(P("region", "tile", None), P("region", "tile")),
        check_vma=False,
    )
```

time: 948 us -> 104 us (0.11)
  the two profiles are of different devices: /device:TPU:8 before, /device:TPU:24 now
where the time goes in v1:
time: 104 us
  Pallas kernels  85.4 us (82%)
  other arithmetic  8.97 us (9%)
  local copies, waits for them, and re-layouts  8.47 us (8%)
    pallas_call x1, Pallas kernels, local(): pl.pallas_call(kernel, name='assemble', out_shape=(jax.ShapeDtypeStruct((...  85.4 us
    unnamed x5, local copies, waits for them, and re-layouts  5.27 us
    convert_element_type x1, other arithmetic, local(): place.astype(BF16)  5.12 us

profile of v1, /device:TPU:24, one launch (start us, length us, event | category | flops | bytes accessed | tf_op | source)
XLA Modules:
  0.0 103.5 jit_solution(8039944440367431997)
XLA Ops:
  0.6 0.9 convert_reduce_fusion
  1.6 0.7 multiply_add_fusion
  2.3 0.6 pad.9
  2.8 0.7 select_reduce_fusion.idx_ref
  3.5 1.6 %fusion.9 = (s32[1]{0:T(128)}, s32[1]{0:T(128)}, s32[1]{0:T(128)}, s32[1]{0:T(128)}, s32[1]{0:T(128)}, /*index=5*/s32[1]{0:T(128)}, s32[1]{0:T(128)}, s32[1]{0:T(128)}) fusion(s32[8]{0:T(128)} %param.15), kind=kLoop, calls=%fused_computation.17 | loop fusion | bytes 64 | tf_op jit(solution)/shard_map/slice | solution.py:350
  5.1 0.8 copy.32
  6.0 0.8 fusion.8
  6.8 0.8 copy.42
  7.6 1.0 copy.41
  8.6 0.9 copy.33
  9.4 5.1 %add_convert_fusion = bf16[192,32]{1,0:T(8,128)(2,1)S(1)} fusion(s32[192,32]{1,0:T(8,128)S(1)} %copy.33, s32[]{:T(128)} %bitcast.9, s32[]{:T(128)} %bitcast.8, s32[]{:T(128)} %bitcast.7, s32[]{:T(128)} %bitcast.6, s32[]{:T(128)} %bitcast.5, s32[]{:T(128)} %bitcast.4, s32[]{:T(128)} %bitcast.3, s32[]{:T(128)} %bitcast.2), kind=kLoop, calls=%fused_computation.13 | loop fusion | flops 147456 | bytes 36896 | tf_op jit(solution)/shard_map/convert_element_type | solution.py:352
  14.6 0.8 fusion.7.aux_ref
  15.3 85.4 %assemble.1 = (f32[1,64,1024]{2,1,0:T(8,128)}, f32[1,64]{1,0:T(1,128)}) custom-call(s32[384]{0:T(512)} %select_reduce_fusion.idx_ref, bf16[192,32,128]{2,1,0:T(8,128)(2,1)} %g_ref.1, bf16[256,256]{1,0:T(8,128)(2,1)} %fusion.7.aux_ref, s32[1,256]{1,0:T(1,128)} %bitcast.14), custom_call_target="tpu_custom_call" | custom-call | tf_op jit(solution)/shard_map/assemble/pallas_call | solution.py:357
  100.8 1.7 %copy.45 = f32[1,64,1024]{2,1,0:T(8,128)} copy(f32[1,64,1024]{2,1,0:T(8,128)} %get-tuple-element.12) | data formatting | bytes 524288
  102.4 1.1 %copy.46 = f32[1,64]{1,0:T(1,128)} copy(f32[1,64]{1,0:T(1,128)} %get-tuple-element.13) | data formatting | bytes 512

commit v2 on v1

--- a/solution.py
+++ b/solution.py
@@ -30,10 +30,7 @@
 )
 
 
-def fit(aux_ref):
-    t = jnp.transpose(aux_ref[...].astype(F32))
-    slopes = [t[32 * c : 32 * c + 32] for c in range(5)]
-    w, r, place = t[160:192], t[192:224], t[224:256]
+def fit(slopes, w, r, place):
     wl = [s * w for s in slopes]
     gamma = [[None] * 5 for _ in range(5)]
     for a in range(5):
@@ -69,10 +66,10 @@
 
 
 def kernel(
-    idx_ref, g_ref, aux_ref, slot_ref,
-    out_ref, vec_ref,
+    place_ref, g_ref, slope_ref, weight_ref, resid_ref, block_ref, count_ref, region_ref,
+    out_ref, vec_ref, idx_ref, idx_vec,
     gsend, grecv, asend, arecv, fitted, lhs, s_buf, d_acc, v_acc, psend, precv, vrecv,
-    gs_sem, gr_sem, as_sem, ar_sem, ps_sem, pr_sem, vs_sem, vr_sem,
+    gs_sem, gr_sem, as_sem, ar_sem, ps_sem, pr_sem, vs_sem, vr_sem, idx_sem,
 ):
     region = lax.axis_index("region")
     tile = lax.axis_index("tile")
@@ -108,11 +105,25 @@
         return carry
 
     lax.fori_loop(0, 16, greet, 0)
-    pl.semaphore_wait(barrier, jnp.where(own_worker, 28, 29))
+    reg = region_ref[...]
+    tracks8 = lax.broadcasted_iota(jnp.int32, (BR, TRK), 0)
+    named = jnp.where(reg == tracks8, 1.0, 0.0)
+    earlier = (
+        lax.broadcasted_iota(jnp.int32, (TRK, TRK), 0) < lax.broadcasted_iota(jnp.int32, (TRK, TRK), 1))
+    ahead = jnp.dot(named.astype(BF16), jnp.where(earlier, 1.0, 0.0).astype(BF16), preferred_element_type=F32)
+    slot = reg.astype(F32) * CAP + jnp.sum(named * ahead, axis=0, keepdims=True)
+    slot_col = jnp.transpose(jnp.broadcast_to(slot, (BR, TRK)))[:, 0:1]
+    slot_lane = lax.broadcasted_iota(jnp.int32, (TRK, N_REGION * CAP), 1).astype(F32)
+    onehot = jnp.where(slot_col == slot_lane, 1.0, 0.0).astype(BF16)
+    number = lax.broadcasted_iota(jnp.int32, (BR, TRK), 1).astype(F32).astype(BF16)
+    idx_vec[...] = jnp.dot(number, onehot, preferred_element_type=F32).astype(jnp.int32)
+    idx_copy = pltpu.make_async_copy(idx_vec.at[pl.ds(0, 1)], idx_ref, idx_sem)
+    idx_copy.start()
+    idx_copy.wait()
 
     def gather(q, ref, k):
         def body(i, carry):
-            ref[k, i] = g_ref[idx_ref[q * HALF + i]]
+            ref[k, i] = g_ref[jnp.clip(idx_ref[0, q * HALF + i], 0, TRK - 1)]
             return carry
         lax.fori_loop(0, HALF, body, 0, unroll=4)
 
@@ -120,19 +131,19 @@
         step, half = DIRS[d][3:]
         return (((colour + step) % 4) * 2 + c) * 2 + half
 
-    def g_copy(d, c):
-        k = d * 2 + c
-        return pltpu.make_async_remote_copy(
-            src_ref=gsend.at[k], dst_ref=grecv.at[d * 2 + core],
-            send_sem=gs_sem.at[k], recv_sem=gr_sem.at[d * 2 + core],
-            device_id=neighbour(d, c))
-
-    def a_copy(d, c):
-        k = d * 2 + c
-        return pltpu.make_async_remote_copy(
-            src_ref=asend.at[k], dst_ref=arecv.at[d * 2 + core],
-            send_sem=as_sem.at[k], recv_sem=ar_sem.at[d * 2 + core],
-            device_id=neighbour(d, c))
+    def g_copy(d, u):
+        k = u * 6 + d
+        return pltpu.make_async_remote_copy(
+            src_ref=gsend.at[k], dst_ref=grecv.at[k],
+            send_sem=gs_sem.at[k], recv_sem=gr_sem.at[k],
+            device_id=neighbour(d, core ^ u))
+
+    def a_copy(d, u):
+        k = u * 6 + d
+        return pltpu.make_async_remote_copy(
+            src_ref=asend.at[k], dst_ref=arecv.at[k],
+            send_sem=as_sem.at[k], recv_sem=ar_sem.at[k],
+            device_id=neighbour(d, core ^ u))
 
     def g_sib(h):
         return pltpu.make_async_remote_copy(
@@ -146,28 +157,36 @@
             send_sem=as_sem.at[12 + h], recv_sem=ar_sem.at[12 + 2 * core + h],
             device_id=sibling)
 
-    for d in range(6):
-        for c in range(2):
-            gather(chunk_of(d, c), gsend, d * 2 + c)
-            g_copy(d, c).start()
+    for u in range(2):
+        for d in range(6):
+            gather(chunk_of(d, core ^ u), gsend, u * 6 + d)
+            if u == 0 and d == 0:
+                pl.semaphore_wait(barrier, jnp.where(own_worker, 28, 29))
+            g_copy(d, u).start()
     for h in range(2):
         gather((colour * 2 + 1 - core) * 2 + h, gsend, 12 + h)
         g_sib(h).start()
     for h in range(2):
         gather((colour * 2 + core) * 2 + h, grecv, 12 + 2 * core + h)
 
-    fitted[...] = fit(aux_ref)
-    slot = slot_ref[...]
+    live = lax.broadcasted_iota(jnp.int32, (HITS, TRK), 0) < count_ref[...]
+    weight = jnp.where(live, weight_ref[...].astype(F32), 0.0)
+    ids = block_ref[...]
+    place = jnp.zeros((HITS, TRK), F32)
+    for b in range(BR):
+        place = jnp.where(ids == b, place_ref[b].astype(F32), place)
+    fitted[...] = fit(
+        [slope_ref[c].astype(F32) for c in range(5)], weight, resid_ref[...].astype(F32), place)
 
     def pick(q):
-        rows = q * HALF + lax.broadcasted_iota(jnp.int32, (HALF, 256), 0)
-        onehot = jnp.where(slot == rows, 1.0, 0.0).astype(BF16)
-        return jnp.dot(onehot, fitted[...], preferred_element_type=F32).astype(BF16)
-
-    for d in range(6):
-        for c in range(2):
-            asend[d * 2 + c] = pick(chunk_of(d, c))
-            a_copy(d, c).start()
+        rows = (q * HALF + lax.broadcasted_iota(jnp.int32, (HALF, TRK), 0)).astype(F32)
+        chosen = jnp.where(slot == rows, 1.0, 0.0).astype(BF16)
+        return jnp.dot(chosen, fitted[...], preferred_element_type=F32).astype(BF16)
+
+    for u in range(2):
+        for d in range(6):
+            asend[u * 6 + d] = pick(chunk_of(d, core ^ u))
+            a_copy(d, u).start()
     for h in range(2):
         asend[12 + h] = pick((colour * 2 + 1 - core) * 2 + h)
         a_sib(h).start()
@@ -258,7 +277,8 @@
     def is_self(i):
         return jnp.logical_and(own_worker, i == tile)
 
-    def piece(a, carry):
+    def piece(s, carry):
+        a = (y + s) % 4
         cols = pl.ds(pl.multiple_of(a * 256, 256), 256)
         prod = lax.dot_general(
             s_buf[:, cols], s_buf[...], (((0,), (0,)), ((), ())), preferred_element_type=F32)
@@ -271,7 +291,7 @@
             for u in range(2):
                 psend[a * 4 + e * 2 + u] = part[ROWS * u : ROWS * u + ROWS]
         for u in range(4):
-            i = a * 4 + u
+            i = a * 4 + (x + u) % 4
 
             @pl.when(jnp.logical_not(is_self(i)))
             def _():
@@ -309,10 +329,10 @@
     row = jnp.sum(jnp.where(mine, vtot, 0.0), axis=0, keepdims=True)
     vec_ref[...] = jnp.where(tile % 2 == 0, row[:, :ROWS], row[:, ROWS:])
 
-    for d in range(6):
-        for c in range(2):
-            g_copy(d, c).wait_send()
-            a_copy(d, c).wait_send()
+    for u in range(2):
+        for d in range(6):
+            g_copy(d, u).wait_send()
+            a_copy(d, u).wait_send()
     for h in range(2):
         g_sib(h).wait_send()
         a_sib(h).wait_send()
@@ -337,21 +357,6 @@
     track_region,
     block_place,
 ):
-    own = track_region[:, 0]
-    order = jnp.arange(TRK)
-    before = (own[:, None] == own[None, :]) & (order[None, :] < order[:, None])
-    slot = own * CAP + jnp.sum(before.astype(jnp.int32), axis=1)
-    slots = jnp.arange(N_REGION * CAP)
-    index = jnp.sum(jnp.where(slot[None, :] == slots[:, None], order[None, :], 0), axis=1).astype(jnp.int32)
-    live = jnp.arange(HITS)[None, :] < hit_count[:, None]
-    weight = jnp.where(live, hit_weight, jnp.zeros_like(hit_weight))
-    place = jnp.zeros(block_ids.shape, jnp.int32)
-    for b in range(BR):
-        place = place + jnp.where(block_ids == b, block_place[b], 0)
-    aux = jnp.concatenate(
-        [local_deriv.reshape(TRK, 5 * HITS), weight, hit_resid, place.astype(BF16)], axis=1)
-    aux = jnp.pad(aux, ((0, 256 - TRK), (0, 0)))
-    slot_row = jnp.pad(slot.astype(jnp.int32), (0, 256 - TRK), constant_values=-1)[None, :]
     vmem = pl.BlockSpec(memory_space=pltpu.VMEM)
     dma = pltpu.SemaphoreType.DMA
     return pl.pallas_call(
@@ -361,14 +366,16 @@
             jax.ShapeDtypeStruct((1, ROWS, WIDTH), F32),
             jax.ShapeDtypeStruct((1, ROWS), F32),
         ),
-        in_specs=[pl.BlockSpec(memory_space=pltpu.SMEM), vmem, vmem, vmem],
+        in_specs=[pl.BlockSpec(memory_space=pltpu.SMEM)] + [vmem] * 7,
         out_specs=(vmem, vmem),
         scratch_shapes=[
+            pltpu.SMEM((1, N_REGION * CAP), jnp.int32),
+            pltpu.VMEM((BR, N_REGION * CAP), jnp.int32),
             pltpu.VMEM((14, HALF, HITS, BS), BF16),
             pltpu.VMEM((CHUNKS, HALF, HITS, BS), BF16),
             pltpu.VMEM((14, HALF, 256), BF16),
             pltpu.VMEM((CHUNKS, HALF, 256), BF16),
-            pltpu.VMEM((256, 256), BF16),
+            pltpu.VMEM((TRK, 256), BF16),
             pltpu.VMEM((WIDTH, HALF * HITS), BF16),
             pltpu.VMEM((CHUNKS * 128, WIDTH), BF16),
             pltpu.VMEM((WIDTH, BS), F32),
@@ -377,11 +384,13 @@
             pltpu.VMEM((16, ROWS, WIDTH), BF16),
             pltpu.VMEM((16, BR, BS), F32),
             dma((14,)), dma((16,)), dma((14,)), dma((16,)),
-            dma((16,)), dma((16,)), dma((16,)), dma((16,)),
+            dma((16,)), dma((16,)), dma((16,)), dma((16,)), dma,
         ],
         compiler_params=pltpu.CompilerParams(
             collective_id=0, has_side_effects=True, vmem_limit_bytes=56 << 20),
-    )(index, global_deriv, aux, slot_row)
+    )(
+        block_place, global_deriv, local_deriv.transpose(1, 2, 0), hit_weight.T, hit_resid.T,
+        block_ids.T, hit_count.reshape(1, TRK), track_region.reshape(1, TRK))
 
 
 def solution(mesh):

time: 104 us -> 69.2 us (0.67)
  the two profiles are of different devices: /device:TPU:24 before, /device:TPU:8 now
where the time goes in v2:
time: 69.2 us; the launch traced here: 68.7 us
  Pallas kernels  65.2 us (94%)
  local copies, waits for them, and re-layouts  2.8 us (4%)
    pallas_call x1, Pallas kernels, local(): pl.pallas_call(kernel, name='assemble', out_shape=(jax.ShapeDtypeStruct((...  65.2 us
    unnamed x2, local copies, waits for them, and re-layouts  2.8 us

profile of v2, /device:TPU:8, one launch (start us, length us, event | category | flops | bytes accessed | tf_op | source)
XLA Modules:
  0.0 68.7 jit_solution(8650633800772857046)
XLA Ops:
  0.6 65.2 %assemble.1 = (f32[1,64,1024]{2,1,0:T(8,128)}, f32[1,64]{1,0:T(1,128)}) custom-call(s32[8]{0:T(128)} %place_ref.1, bf16[192,32,128]{2,1,0:T(8,128)(2,1)} %g_ref.1, bf16[5,32,192]{2,1,0:T(8,128)(2,1)} %bitcast.6, bf16[32,192]{1,0:T(8,128)(2,1)} %bitcast.8, bf16[32,192]{1,0:T(8,128)(2,1)} %bitcast.9, s32[32,192]{1,0:T(8,128)} %bitcast.7, s32[1,192]{1,0:T(1,128)} %bitcast.10, ...), custom_call_target="tpu_custom_call" | custom-call | tf_op jit(solution)/shard_map/assemble/pallas_call | solution.py:362
  65.9 1.7 %copy.12 = f32[1,64,1024]{2,1,0:T(8,128)} copy(f32[1,64,1024]{2,1,0:T(8,128)} %get-tuple-element.4) | data formatting | bytes 524288
  67.5 1.1 %copy.13 = f32[1,64]{1,0:T(1,128)} copy(f32[1,64]{1,0:T(1,128)} %get-tuple-element.5) | data formatting | bytes 512

commit v3 on v2

--- a/solution.py
+++ b/solution.py
@@ -68,8 +68,9 @@
 def kernel(
     place_ref, g_ref, slope_ref, weight_ref, resid_ref, block_ref, count_ref, region_ref,
     out_ref, vec_ref, idx_ref, idx_vec,
-    gsend, grecv, asend, arecv, fitted, lhs, s_buf, d_acc, v_acc, psend, precv, vrecv,
-    gs_sem, gr_sem, as_sem, ar_sem, ps_sem, pr_sem, vs_sem, vr_sem, idx_sem,
+    gsend, grecv, asend, arecv, fitted, lhs, wp_buf, s_buf, d_acc, v_acc,
+    psend, precv, vrecv, dsend, drecv, xsend, xrecv,
+    gs_sem, gr_sem, as_sem, ar_sem, ps_sem, pr_sem, vs_sem, vr_sem, ds_sem, dr_sem, xs_sem, xr_sem, idx_sem,
 ):
     region = lax.axis_index("region")
     tile = lax.axis_index("tile")
@@ -105,6 +106,20 @@
         return carry
 
     lax.fori_loop(0, 16, greet, 0)
+    mine = tile // 2
+
+    def owner(a, e):
+        return {"region": region, "tile": ((a + 8) % 8) * 2 + e}
+
+    for j in range(1, 4):
+        for e in range(2):
+            pl.semaphore_signal(barrier, inc=1, device_id=owner(mine - j, e))
+
+    @pl.when(mine >= 4)
+    def _():
+        for e in range(2):
+            pl.semaphore_signal(barrier, inc=1, device_id=owner(mine - 4, e))
+
     reg = region_ref[...]
     tracks8 = lax.broadcasted_iota(jnp.int32, (BR, TRK), 0)
     named = jnp.where(reg == tracks8, 1.0, 0.0)
@@ -157,17 +172,15 @@
             send_sem=as_sem.at[12 + h], recv_sem=ar_sem.at[12 + 2 * core + h],
             device_id=sibling)
 
-    for u in range(2):
+    def send_tracks(u):
         for d in range(6):
             gather(chunk_of(d, core ^ u), gsend, u * 6 + d)
             if u == 0 and d == 0:
-                pl.semaphore_wait(barrier, jnp.where(own_worker, 28, 29))
+                pl.semaphore_wait(
+                    barrier, jnp.where(own_worker, 34, 35) + jnp.where(mine < 4, 2, 0))
             g_copy(d, u).start()
-    for h in range(2):
-        gather((colour * 2 + 1 - core) * 2 + h, gsend, 12 + h)
-        g_sib(h).start()
-    for h in range(2):
-        gather((colour * 2 + core) * 2 + h, grecv, 12 + 2 * core + h)
+
+    send_tracks(0)
 
     live = lax.broadcasted_iota(jnp.int32, (HITS, TRK), 0) < count_ref[...]
     weight = jnp.where(live, weight_ref[...].astype(F32), 0.0)
@@ -190,10 +203,14 @@
     for h in range(2):
         asend[12 + h] = pick((colour * 2 + 1 - core) * 2 + h)
         a_sib(h).start()
+    send_tracks(1)
+    for h in range(2):
+        gather((colour * 2 + 1 - core) * 2 + h, gsend, 12 + h)
+        g_sib(h).start()
     for h in range(2):
         arecv[12 + 2 * core + h] = pick((colour * 2 + core) * 2 + h)
-
-    d_acc[...] = jnp.zeros_like(d_acc)
+        gather((colour * 2 + core) * 2 + h, grecv, 12 + 2 * core + h)
+
     v_acc[...] = jnp.zeros_like(v_acc)
 
     lane = lax.broadcasted_iota(jnp.int32, (GROUP, 128), 1)
@@ -202,8 +219,11 @@
     blocks = [(lane // HITS + 4 * v) == track for v in range(2)]
     subf = lax.broadcasted_iota(jnp.int32, (GROUP, 256), 0).astype(F32)
 
+    def chunk_at(m):
+        return jnp.where(m < 2, 12 + 2 * core + m, jnp.where(m < 4, 12 + 2 * (1 - core) + m - 2, m - 4))
+
     def chunk(m, carry):
-        n = jnp.where(m < 2, 12 + 2 * core + m, jnp.where(m < 4, 12 + 2 * (1 - core) + m - 2, m - 4))
+        n = chunk_at(m)
 
         @pl.when(m >= 2)
         def _():
@@ -216,7 +236,6 @@
 
         a = arecv[n].astype(F32)
         g = grecv[n].reshape(HALF * HITS, BS)
-        gt = jnp.transpose(g)
         parts, wps = [], []
         vec = None
         for j in range(3):
@@ -251,51 +270,66 @@
             vec = vj if vec is None else vec + vj
             wps.append(jnp.where(onp, wrow, 0.0).astype(BF16))
         v_acc[...] += vec
-        wp = jnp.concatenate(wps, axis=1)
+        wp_buf[m] = jnp.concatenate(wps, axis=1)
         pad = jnp.zeros((8, BS), F32)
+        rows = pl.ds(pl.multiple_of(m * 128, 128), 128)
         for p in range(BR):
-            piece = jnp.concatenate([q[40 * p : 40 * p + 40] for q in parts] + [pad], axis=0)
-            s_buf[pl.ds(pl.multiple_of(m * 128, 128), 128), BS * p : BS * p + BS] = piece.astype(BF16)
-            lhs[BS * p : BS * p + BS, :] = gt * wp[p : p + 1, :]
-        d_acc[...] += jnp.dot(lhs[...], g, preferred_element_type=F32)
+            piece = jnp.concatenate([q[40 * p : 40 * p + 40] for q in parts] + [pad], axis=0).astype(BF16)
+            s_buf[rows, BS * p : BS * p + BS] = piece
+            if p < 4:
+                s_buf[rows, WIDTH + BS * p : WIDTH + BS * p + BS] = piece
         return carry
 
     lax.fori_loop(0, CHUNKS, chunk, 0)
 
-    def p_copy(i):
-        return pltpu.make_async_remote_copy(
-            src_ref=psend.at[i], dst_ref=precv.at[tile],
-            send_sem=ps_sem.at[i], recv_sem=pr_sem.at[tile],
-            device_id={"region": colour * 2 + core, "tile": i})
+    def target(i):
+        return {"region": colour * 2 + core, "tile": i}
+
+    def p_copy(i, count):
+        return pltpu.make_async_remote_copy(
+            src_ref=psend.at[i, pl.ds(0, count)], dst_ref=precv.at[tile, pl.ds(0, count)],
+            send_sem=ps_sem.at[i], recv_sem=pr_sem.at[tile], device_id=target(i))
 
     def v_copy(i):
         return pltpu.make_async_remote_copy(
             src_ref=v_acc, dst_ref=vrecv.at[tile],
-            send_sem=vs_sem.at[i], recv_sem=vr_sem.at[tile],
-            device_id={"region": colour * 2 + core, "tile": i})
+            send_sem=vs_sem.at[i], recv_sem=vr_sem.at[tile], device_id=target(i))
+
+    def d_copy(i):
+        return pltpu.make_async_remote_copy(
+            src_ref=dsend.at[i], dst_ref=drecv.at[tile],
+            send_sem=ds_sem.at[i], recv_sem=dr_sem.at[tile], device_id=target(i))
 
     def is_self(i):
         return jnp.logical_and(own_worker, i == tile)
 
     def piece(s, carry):
-        a = (y + s) % 4
-        cols = pl.ds(pl.multiple_of(a * 256, 256), 256)
+        yy = (y + s) % 4
+        cols = pl.ds(pl.multiple_of(yy * 256, 256), 256)
+        wide = pl.ds(pl.multiple_of(yy * 256, 256), 768)
         prod = lax.dot_general(
-            s_buf[:, cols], s_buf[...], (((0,), (0,)), ((), ())), preferred_element_type=F32)
-        lhs_cols = lax.broadcasted_iota(jnp.int32, (1, WIDTH), 1) // BS
-        for e in range(2):
-            dblock = d_acc[pl.ds(pl.multiple_of(a * 256 + e * 128, 128), 128), :]
-            wide = jnp.concatenate([dblock] * BR, axis=1)
-            part = jnp.where(lhs_cols == a * 2 + e, wide, 0.0) - prod[e * 128 : e * 128 + 128]
+            s_buf[:, cols], s_buf[:, wide], (((0,), (0,)), ((), ())), preferred_element_type=F32)
+        for e in range(2):
+            part = -prod[128 * e : 128 * e + 128, 128 * e : 128 * e + 640]
+            d_acc[pl.ds(pl.multiple_of(yy * 256 + 128 * e, 128), 128), :] = part[:, :128]
             part = part.astype(BF16)
             for u in range(2):
-                psend[a * 4 + e * 2 + u] = part[ROWS * u : ROWS * u + ROWS]
+                for j in range(4):
+                    psend[yy * 4 + e * 2 + u, j] = part[ROWS * u : ROWS * u + ROWS, BS * (j + 1) : BS * (j + 2)]
         for u in range(4):
-            i = a * 4 + (x + u) % 4
-
-            @pl.when(jnp.logical_not(is_self(i)))
+            i = yy * 4 + (x + u) % 4
+            other = jnp.logical_not(is_self(i))
+
+            @pl.when(jnp.logical_and(other, yy < 2))
             def _():
-                p_copy(i).start()
+                p_copy(i, 4).start()
+
+            @pl.when(jnp.logical_and(other, yy >= 2))
+            def _():
+                p_copy(i, 3).start()
+
+            @pl.when(other)
+            def _():
                 v_copy(i).start()
 
             @pl.when(is_self(i))
@@ -306,12 +340,51 @@
 
     lax.fori_loop(0, 4, piece, 0)
 
+    def diagonal(m, carry):
+        g = grecv[chunk_at(m)].reshape(HALF * HITS, BS)
+        gt = jnp.transpose(g)
+        wp = wp_buf[m]
+        for p in range(BR):
+            lhs[BS * p : BS * p + BS, :] = gt * wp[p : p + 1, :]
+        d_acc[...] += jnp.dot(lhs[...], g, preferred_element_type=F32)
+        return carry
+
+    lax.fori_loop(0, CHUNKS, diagonal, 0)
+
+    def send_diagonal(s, carry):
+        yy = (y + s // 4) % 4
+        i = yy * 4 + (x + s) % 4
+        dsend[i] = d_acc[pl.ds(pl.multiple_of(i * ROWS, ROWS), ROWS), :].astype(BF16)
+
+        @pl.when(jnp.logical_not(is_self(i)))
+        def _():
+            d_copy(i).start()
+
+        @pl.when(is_self(i))
+        def _():
+            drecv[tile] = dsend[i]
+        return carry
+
+    lax.fori_loop(0, 16, send_diagonal, 0)
+
+    def p_arrival(i, count):
+        return pltpu.make_async_remote_copy(
+            src_ref=psend.at[0, pl.ds(0, count)], dst_ref=precv.at[i, pl.ds(0, count)],
+            send_sem=ps_sem.at[0], recv_sem=pr_sem.at[i], device_id=sibling)
+
     def collect(i, carry):
-        @pl.when(jnp.logical_not(is_self(i)))
-        def _():
-            pltpu.make_async_remote_copy(
-                src_ref=psend.at[0], dst_ref=precv.at[i], send_sem=ps_sem.at[0],
-                recv_sem=pr_sem.at[i], device_id=sibling).wait_recv()
+        other = jnp.logical_not(is_self(i))
+
+        @pl.when(jnp.logical_and(other, mine < 4))
+        def _():
+            p_arrival(i, 4).wait_recv()
+
+        @pl.when(jnp.logical_and(other, mine >= 4))
+        def _():
+            p_arrival(i, 3).wait_recv()
+
+        @pl.when(other)
+        def _():
             pltpu.make_async_remote_copy(
                 src_ref=v_acc, dst_ref=vrecv.at[i], send_sem=vs_sem.at[0],
                 recv_sem=vr_sem.at[i], device_id=sibling).wait_recv()
@@ -319,15 +392,82 @@
 
     lax.fori_loop(0, 16, collect, 0)
 
-    total = precv[0].astype(F32)
+    def x_copy(j, e):
+        k = 2 * j - 2 + e
+        return pltpu.make_async_remote_copy(
+            src_ref=xsend.at[k], dst_ref=xrecv.at[2 * j - 2 + tile % 2],
+            send_sem=xs_sem.at[k], recv_sem=xr_sem.at[2 * j - 2 + tile % 2], device_id=owner(mine + j, e))
+
+    def x_arrival(j, e):
+        k = 2 * j - 2 + e
+        return pltpu.make_async_remote_copy(
+            src_ref=xsend.at[k], dst_ref=xrecv.at[k],
+            send_sem=xs_sem.at[k], recv_sem=xr_sem.at[k], device_id=sibling)
+
+    def column(b):
+        return pl.ds(pl.multiple_of(((b + 8) % 8) * BS, BS), BS)
+
+    def reduce_block(j):
+        total = precv[0, j - 1].astype(F32)
+        for i in range(1, 16):
+            total = total + precv[i, j - 1].astype(F32)
+        out_ref[0, :, column(mine + j)] = total
+        turned = jnp.transpose(total)
+        for e in range(2):
+            t = turned[ROWS * e : ROWS * e + ROWS]
+            xsend[2 * j - 2 + e] = jnp.concatenate([t[:32], t[32:]], axis=1)
+            x_copy(j, e).start()
+
+    def receive_block(j):
+        for e in range(2):
+            x_arrival(j, e).wait_recv()
+        q0, q1 = xrecv[2 * j - 2], xrecv[2 * j - 1]
+        out_ref[0, 0:32, column(mine - j)] = jnp.concatenate([q0[:, :ROWS], q1[:, :ROWS]], axis=1)
+        out_ref[0, 32:64, column(mine - j)] = jnp.concatenate([q0[:, ROWS:], q1[:, ROWS:]], axis=1)
+
+    @pl.when(mine < 4)
+    def _():
+        reduce_block(4)
+
+    for j in range(3, 0, -1):
+        reduce_block(j)
+
     vtot = vrecv[0]
     for i in range(1, 16):
-        total = total + precv[i].astype(F32)
         vtot = vtot + vrecv[i]
-    out_ref[0] = total
-    mine = lax.broadcasted_iota(jnp.int32, (BR, BS), 0) == tile // 2
-    row = jnp.sum(jnp.where(mine, vtot, 0.0), axis=0, keepdims=True)
+    here = lax.broadcasted_iota(jnp.int32, (BR, BS), 0) == mine
+    row = jnp.sum(jnp.where(here, vtot, 0.0), axis=0, keepdims=True)
     vec_ref[...] = jnp.where(tile % 2 == 0, row[:, :ROWS], row[:, ROWS:])
+
+    def collect_diagonal(i, carry):
+        @pl.when(jnp.logical_not(is_self(i)))
+        def _():
+            pltpu.make_async_remote_copy(
+                src_ref=dsend.at[0], dst_ref=drecv.at[i], send_sem=ds_sem.at[0],
+                recv_sem=dr_sem.at[i], device_id=sibling).wait_recv()
+        return carry
+
+    lax.fori_loop(0, 16, collect_diagonal, 0)
+    total = drecv[0].astype(F32)
+    for i in range(1, 16):
+        total = total + drecv[i].astype(F32)
+    out_ref[0, :, column(mine)] = total
+
+    for j in range(1, 4):
+        receive_block(j)
+
+    @pl.when(mine >= 4)
+    def _():
+        receive_block(4)
+
+    for j in range(1, 4):
+        for e in range(2):
+            x_copy(j, e).wait_send()
+
+    @pl.when(mine < 4)
+    def _():
+        for e in range(2):
+            x_copy(4, e).wait_send()
 
     for u in range(2):
         for d in range(6):
@@ -338,10 +478,20 @@
         a_sib(h).wait_send()
 
     def finish(i, carry):
-        @pl.when(jnp.logical_not(is_self(i)))
-        def _():
-            p_copy(i).wait_send()
+        other = jnp.logical_not(is_self(i))
+
+        @pl.when(jnp.logical_and(other, i < 8))
+        def _():
+            p_copy(i, 4).wait_send()
+
+        @pl.when(jnp.logical_and(other, i >= 8))
+        def _():
+            p_copy(i, 3).wait_send()
+
+        @pl.when(other)
+        def _():
             v_copy(i).wait_send()
+            d_copy(i).wait_send()
         return carry
 
     lax.fori_loop(0, 16, finish, 0)
@@ -377,14 +527,19 @@
             pltpu.VMEM((CHUNKS, HALF, 256), BF16),
             pltpu.VMEM((TRK, 256), BF16),
             pltpu.VMEM((WIDTH, HALF * HITS), BF16),
-            pltpu.VMEM((CHUNKS * 128, WIDTH), BF16),
+            pltpu.VMEM((CHUNKS, BR, HALF * HITS), BF16),
+            pltpu.VMEM((CHUNKS * 128, WIDTH + WIDTH // 2), BF16),
             pltpu.VMEM((WIDTH, BS), F32),
             pltpu.VMEM((BR, BS), F32),
-            pltpu.VMEM((16, ROWS, WIDTH), BF16),
-            pltpu.VMEM((16, ROWS, WIDTH), BF16),
+            pltpu.VMEM((16, 4, ROWS, BS), BF16),
+            pltpu.VMEM((16, 4, ROWS, BS), BF16),
             pltpu.VMEM((16, BR, BS), F32),
+            pltpu.VMEM((16, ROWS, BS), BF16),
+            pltpu.VMEM((16, ROWS, BS), BF16),
+            pltpu.VMEM((8, 32, BS), F32),
+            pltpu.VMEM((8, 32, BS), F32),
             dma((14,)), dma((16,)), dma((14,)), dma((16,)),
-            dma((16,)), dma((16,)), dma((16,)), dma((16,)), dma,
+            dma((16,)), dma((16,)), dma((16,)), dma((16,)), dma((16,)), dma((16,)), dma((8,)), dma((8,)), dma,
         ],
         compiler_params=pltpu.CompilerParams(
             collective_id=0, has_side_effects=True, vmem_limit_bytes=56 << 20),

time: 69.2 us -> 53.4 us (0.77)
  Pallas kernels: 65.2 us -> 49.6 us
    pallas_call x1, Pallas kernels: 65.2 us -> 49.6 us  [local(): pl.pallas_call(kernel, name='assemble', out_shape=(jax.ShapeDtypeStruct((...]
where the time goes in v3:
time: 53.4 us; the launch traced here: 53.1 us
  Pallas kernels  49.6 us (93%)
  local copies, waits for them, and re-layouts  2.8 us (5%)
  between operations  0.64 us (1%)
    pallas_call x1, Pallas kernels, local(): pl.pallas_call(kernel, name='assemble', out_shape=(jax.ShapeDtypeStruct((...  49.6 us
    unnamed x2, local copies, waits for them, and re-layouts  2.8 us

profile of v3, /device:TPU:8, one launch (start us, length us, event | category | flops | bytes accessed | tf_op | source)
XLA Modules:
  0.0 53.1 jit_solution(9104093772193279834)
XLA Ops:
  0.6 49.6 %assemble.1 = (f32[1,64,1024]{2,1,0:T(8,128)}, f32[1,64]{1,0:T(1,128)}) custom-call(s32[8]{0:T(128)} %place_ref.1, bf16[192,32,128]{2,1,0:T(8,128)(2,1)} %g_ref.1, bf16[5,32,192]{2,1,0:T(8,128)(2,1)} %bitcast.6, bf16[32,192]{1,0:T(8,128)(2,1)} %bitcast.8, bf16[32,192]{1,0:T(8,128)(2,1)} %bitcast.9, s32[32,192]{1,0:T(8,128)} %bitcast.7, s32[1,192]{1,0:T(1,128)} %bitcast.10, ...), custom_call_target="tpu_custom_call" | custom-call | tf_op jit(solution)/shard_map/assemble/pallas_call | solution.py:512
  50.3 1.7 %copy.12 = f32[1,64,1024]{2,1,0:T(8,128)} copy(f32[1,64,1024]{2,1,0:T(8,128)} %get-tuple-element.4) | data formatting | bytes 524288
  51.9 1.1 %copy.13 = f32[1,64]{1,0:T(1,128)} copy(f32[1,64]{1,0:T(1,128)} %get-tuple-element.5) | data formatting | bytes 512

commit v4 on v3

--- a/solution.py
+++ b/solution.py
@@ -68,7 +68,7 @@
 def kernel(
     place_ref, g_ref, slope_ref, weight_ref, resid_ref, block_ref, count_ref, region_ref,
     out_ref, vec_ref, idx_ref, idx_vec,
-    gsend, grecv, asend, arecv, fitted, lhs, wp_buf, s_buf, d_acc, v_acc,
+    gsend, grecv, asend, arecv, fitted, lhs, wp_buf, s_buf, p_acc, d_acc, v_acc, vsend,
     psend, precv, vrecv, dsend, drecv, xsend, xrecv,
     gs_sem, gr_sem, as_sem, ar_sem, ps_sem, pr_sem, vs_sem, vr_sem, ds_sem, dr_sem, xs_sem, xr_sem, idx_sem,
 ):
@@ -136,21 +136,19 @@
     idx_copy.start()
     idx_copy.wait()
 
-    def gather(q, ref, k):
-        def body(i, carry):
-            ref[k, i] = g_ref[jnp.clip(idx_ref[0, q * HALF + i], 0, TRK - 1)]
-            return carry
-        lax.fori_loop(0, HALF, body, 0, unroll=4)
+    def gather(q, t, ref, k):
+        for i in range(GROUP):
+            ref[k, t, i] = g_ref[jnp.clip(idx_ref[0, q * HALF + t * GROUP + i], 0, TRK - 1)]
 
     def chunk_of(d, c):
         step, half = DIRS[d][3:]
         return (((colour + step) % 4) * 2 + c) * 2 + half
 
-    def g_copy(d, u):
+    def g_copy(d, u, t):
         k = u * 6 + d
         return pltpu.make_async_remote_copy(
-            src_ref=gsend.at[k], dst_ref=grecv.at[k],
-            send_sem=gs_sem.at[k], recv_sem=gr_sem.at[k],
+            src_ref=gsend.at[k, t], dst_ref=grecv.at[k, t],
+            send_sem=gs_sem.at[k, t], recv_sem=gr_sem.at[k, t],
             device_id=neighbour(d, core ^ u))
 
     def a_copy(d, u):
@@ -160,10 +158,10 @@
             send_sem=as_sem.at[k], recv_sem=ar_sem.at[k],
             device_id=neighbour(d, core ^ u))
 
-    def g_sib(h):
-        return pltpu.make_async_remote_copy(
-            src_ref=gsend.at[12 + h], dst_ref=grecv.at[12 + 2 * core + h],
-            send_sem=gs_sem.at[12 + h], recv_sem=gr_sem.at[12 + 2 * core + h],
+    def g_sib(h, t):
+        return pltpu.make_async_remote_copy(
+            src_ref=gsend.at[12 + h, t], dst_ref=grecv.at[12 + 2 * core + h, t],
+            send_sem=gs_sem.at[12 + h, t], recv_sem=gr_sem.at[12 + 2 * core + h, t],
             device_id=sibling)
 
     def a_sib(h):
@@ -173,12 +171,13 @@
             device_id=sibling)
 
     def send_tracks(u):
-        for d in range(6):
-            gather(chunk_of(d, core ^ u), gsend, u * 6 + d)
-            if u == 0 and d == 0:
-                pl.semaphore_wait(
-                    barrier, jnp.where(own_worker, 34, 35) + jnp.where(mine < 4, 2, 0))
-            g_copy(d, u).start()
+        for t in range(3):
+            for d in range(6):
+                gather(chunk_of(d, core ^ u), t, gsend, u * 6 + d)
+                if u == 0 and t == 0 and d == 0:
+                    pl.semaphore_wait(
+                        barrier, jnp.where(own_worker, 34, 35) + jnp.where(mine < 4, 2, 0))
+                g_copy(d, u, t).start()
 
     send_tracks(0)
 
@@ -191,25 +190,29 @@
     fitted[...] = fit(
         [slope_ref[c].astype(F32) for c in range(5)], weight, resid_ref[...].astype(F32), place)
 
-    def pick(q):
+    def pick(q, ref, k):
         rows = (q * HALF + lax.broadcasted_iota(jnp.int32, (HALF, TRK), 0)).astype(F32)
         chosen = jnp.where(slot == rows, 1.0, 0.0).astype(BF16)
-        return jnp.dot(chosen, fitted[...], preferred_element_type=F32).astype(BF16)
+        picked = jnp.dot(chosen, fitted[...], preferred_element_type=F32)
+        for t in range(3):
+            ref[k, t] = picked[GROUP * t : GROUP * t + GROUP].astype(BF16)
 
     for u in range(2):
         for d in range(6):
-            asend[u * 6 + d] = pick(chunk_of(d, core ^ u))
+            pick(chunk_of(d, core ^ u), asend, u * 6 + d)
             a_copy(d, u).start()
     for h in range(2):
-        asend[12 + h] = pick((colour * 2 + 1 - core) * 2 + h)
+        pick((colour * 2 + 1 - core) * 2 + h, asend, 12 + h)
         a_sib(h).start()
     send_tracks(1)
     for h in range(2):
-        gather((colour * 2 + 1 - core) * 2 + h, gsend, 12 + h)
-        g_sib(h).start()
+        for t in range(3):
+            gather((colour * 2 + 1 - core) * 2 + h, t, gsend, 12 + h)
+            g_sib(h, t).start()
     for h in range(2):
-        arecv[12 + 2 * core + h] = pick((colour * 2 + core) * 2 + h)
-        gather((colour * 2 + core) * 2 + h, grecv, 12 + 2 * core + h)
+        pick((colour * 2 + core) * 2 + h, arecv, 12 + 2 * core + h)
+        for t in range(3):
+            gather((colour * 2 + core) * 2 + h, t, grecv, 12 + 2 * core + h)
 
     v_acc[...] = jnp.zeros_like(v_acc)
 
@@ -219,28 +222,42 @@
     blocks = [(lane // HITS + 4 * v) == track for v in range(2)]
     subf = lax.broadcasted_iota(jnp.int32, (GROUP, 256), 0).astype(F32)
 
-    def chunk_at(m):
-        return jnp.where(m < 2, 12 + 2 * core + m, jnp.where(m < 4, 12 + 2 * (1 - core) + m - 2, m - 4))
-
-    def chunk(m, carry):
-        n = chunk_at(m)
-
-        @pl.when(m >= 2)
-        def _():
+    def group_of(m, q):
+        far = m - 2
+        source = jnp.where(m == 0, core, 1 - core)
+        k = jnp.where(m < 2, 12 + 2 * source + q // 3, far // 3 * 6 + q)
+        return k, jnp.where(m < 2, q % 3, far % 3)
+
+    def batch(m, carry):
+        found = [group_of(m, q) for q in range(6)]
+
+        @pl.when(m >= 1)
+        def _():
+            for k, t in found:
+                pltpu.make_async_remote_copy(
+                    src_ref=gsend.at[0, 0], dst_ref=grecv.at[k, t], send_sem=gs_sem.at[0, 0],
+                    recv_sem=gr_sem.at[k, t], device_id=sibling).wait_recv()
+
+        def aux_arrival(k):
             pltpu.make_async_remote_copy(
-                src_ref=gsend.at[0], dst_ref=grecv.at[n], send_sem=gs_sem.at[0],
-                recv_sem=gr_sem.at[n], device_id=sibling).wait_recv()
-            pltpu.make_async_remote_copy(
-                src_ref=asend.at[0], dst_ref=arecv.at[n], send_sem=as_sem.at[0],
-                recv_sem=ar_sem.at[n], device_id=sibling).wait_recv()
-
-        a = arecv[n].astype(F32)
-        g = grecv[n].reshape(HALF * HITS, BS)
+                src_ref=asend.at[0], dst_ref=arecv.at[k], send_sem=as_sem.at[0],
+                recv_sem=ar_sem.at[k], device_id=sibling).wait_recv()
+
+        @pl.when(m == 1)
+        def _():
+            for h in range(2):
+                aux_arrival(12 + 2 * (1 - core) + h)
+
+        @pl.when(jnp.logical_and(m >= 2, (m - 2) % 3 == 0))
+        def _():
+            for d in range(6):
+                aux_arrival((m - 2) // 3 * 6 + d)
+
         parts, wps = [], []
         vec = None
-        for j in range(3):
-            aj = a[GROUP * j : GROUP * j + GROUP]
-
+        for k, t in found:
+            aj = arecv[k, t].astype(F32)
+            gj = grecv[k, t].reshape(GROUP * HITS, BS)
             turned = []
             for v in range(2):
                 half = aj[:, 128 * v : 128 * v + 128]
@@ -260,7 +277,6 @@
                 here = place == float(p)
                 rows.extend(jnp.where(here, b, 0.0) for b in base)
             left = jnp.concatenate(rows, axis=0).astype(BF16)
-            gj = g[256 * j : 256 * j + 256]
             parts.append(jnp.dot(left, gj, preferred_element_type=F32))
             prow = jnp.sum(place, axis=0, keepdims=True)
             hrow = jnp.sum(spread_lanes(5), axis=0, keepdims=True)
@@ -270,17 +286,34 @@
             vec = vj if vec is None else vec + vj
             wps.append(jnp.where(onp, wrow, 0.0).astype(BF16))
         v_acc[...] += vec
-        wp_buf[m] = jnp.concatenate(wps, axis=1)
-        pad = jnp.zeros((8, BS), F32)
-        rows = pl.ds(pl.multiple_of(m * 128, 128), 128)
+        for h in range(2):
+            wp_buf[2 * m + h] = jnp.concatenate(wps[3 * h : 3 * h + 3], axis=1)
+        rows = pl.ds(pl.multiple_of(m * 240, 16), 240)
         for p in range(BR):
-            piece = jnp.concatenate([q[40 * p : 40 * p + 40] for q in parts] + [pad], axis=0).astype(BF16)
+            piece = jnp.concatenate([q[40 * p : 40 * p + 40] for q in parts], axis=0).astype(BF16)
             s_buf[rows, BS * p : BS * p + BS] = piece
             if p < 4:
                 s_buf[rows, WIDTH + BS * p : WIDTH + BS * p + BS] = piece
         return carry
 
-    lax.fori_loop(0, CHUNKS, chunk, 0)
+    def product(yy, first, count):
+        start = pl.multiple_of(yy * 256, 256)
+        return lax.dot_general(
+            s_buf[first : first + count, pl.ds(start, 256)], s_buf[first : first + count, pl.ds(start, 768)],
+            (((0,), (0,)), ((), ())), preferred_element_type=F32)
+
+    def accumulate(first, count):
+        def body(yy, carry):
+            p = product(yy, first, count)
+            p_acc[yy] = p if first == 0 else p_acc[yy] + p
+            return carry
+        lax.fori_loop(0, 4, body, 0)
+
+    lax.fori_loop(0, 2, batch, 0)
+    accumulate(0, 480)
+    lax.fori_loop(2, 5, batch, 0)
+    accumulate(480, 720)
+    lax.fori_loop(5, 8, batch, 0)
 
     def target(i):
         return {"region": colour * 2 + core, "tile": i}
@@ -292,7 +325,7 @@
 
     def v_copy(i):
         return pltpu.make_async_remote_copy(
-            src_ref=v_acc, dst_ref=vrecv.at[tile],
+            src_ref=vsend.at[i // 2], dst_ref=vrecv.at[tile],
             send_sem=vs_sem.at[i], recv_sem=vr_sem.at[tile], device_id=target(i))
 
     def d_copy(i):
@@ -303,12 +336,15 @@
     def is_self(i):
         return jnp.logical_and(own_worker, i == tile)
 
+    for p in range(BR):
+        vsend[p] = v_acc[p : p + 1, :]
+
+    def turn(s):
+        return jnp.where(s == 0, 1, jnp.where(s == 1, 3, jnp.where(s == 2, 2, 0)))
+
     def piece(s, carry):
-        yy = (y + s) % 4
-        cols = pl.ds(pl.multiple_of(yy * 256, 256), 256)
-        wide = pl.ds(pl.multiple_of(yy * 256, 256), 768)
-        prod = lax.dot_general(
-            s_buf[:, cols], s_buf[:, wide], (((0,), (0,)), ((), ())), preferred_element_type=F32)
+        yy = (y + turn(s)) % 4
+        prod = p_acc[yy] + product(yy, 1200, 720)
         for e in range(2):
             part = -prod[128 * e : 128 * e + 128, 128 * e : 128 * e + 640]
             d_acc[pl.ds(pl.multiple_of(yy * 256 + 128 * e, 128), 128), :] = part[:, :128]
@@ -316,7 +352,7 @@
             for u in range(2):
                 for j in range(4):
                     psend[yy * 4 + e * 2 + u, j] = part[ROWS * u : ROWS * u + ROWS, BS * (j + 1) : BS * (j + 2)]
-        for u in range(4):
+        for u in (1, 3, 2, 0):
             i = yy * 4 + (x + u) % 4
             other = jnp.logical_not(is_self(i))
 
@@ -335,13 +371,14 @@
             @pl.when(is_self(i))
             def _():
                 precv[tile] = psend[i]
-                vrecv[tile] = v_acc[...]
+                vrecv[tile] = vsend[i // 2]
         return carry
 
     lax.fori_loop(0, 4, piece, 0)
 
     def diagonal(m, carry):
-        g = grecv[chunk_at(m)].reshape(HALF * HITS, BS)
+        found = [group_of(m // 2, m % 2 * 3 + q) for q in range(3)]
+        g = jnp.concatenate([grecv[k, t].reshape(GROUP * HITS, BS) for k, t in found], axis=0)
         gt = jnp.transpose(g)
         wp = wp_buf[m]
         for p in range(BR):
@@ -352,8 +389,7 @@
     lax.fori_loop(0, CHUNKS, diagonal, 0)
 
     def send_diagonal(s, carry):
-        yy = (y + s // 4) % 4
-        i = yy * 4 + (x + s) % 4
+        i = (y + turn(s // 4)) % 4 * 4 + (x + turn(s % 4)) % 4
         dsend[i] = d_acc[pl.ds(pl.multiple_of(i * ROWS, ROWS), ROWS), :].astype(BF16)
 
         @pl.when(jnp.logical_not(is_self(i)))
@@ -386,7 +422,7 @@
         @pl.when(other)
         def _():
             pltpu.make_async_remote_copy(
-                src_ref=v_acc, dst_ref=vrecv.at[i], send_sem=vs_sem.at[0],
+                src_ref=vsend.at[0], dst_ref=vrecv.at[i], send_sem=vs_sem.at[0],
                 recv_sem=vr_sem.at[i], device_id=sibling).wait_recv()
         return carry
 
@@ -415,13 +451,13 @@
         turned = jnp.transpose(total)
         for e in range(2):
             t = turned[ROWS * e : ROWS * e + ROWS]
-            xsend[2 * j - 2 + e] = jnp.concatenate([t[:32], t[32:]], axis=1)
+            xsend[2 * j - 2 + e] = jnp.concatenate([t[:32], t[32:]], axis=1).astype(BF16)
             x_copy(j, e).start()
 
     def receive_block(j):
         for e in range(2):
             x_arrival(j, e).wait_recv()
-        q0, q1 = xrecv[2 * j - 2], xrecv[2 * j - 1]
+        q0, q1 = xrecv[2 * j - 2].astype(F32), xrecv[2 * j - 1].astype(F32)
         out_ref[0, 0:32, column(mine - j)] = jnp.concatenate([q0[:, :ROWS], q1[:, :ROWS]], axis=1)
         out_ref[0, 32:64, column(mine - j)] = jnp.concatenate([q0[:, ROWS:], q1[:, ROWS:]], axis=1)
 
@@ -432,11 +468,9 @@
     for j in range(3, 0, -1):
         reduce_block(j)
 
-    vtot = vrecv[0]
+    row = vrecv[0]
     for i in range(1, 16):
-        vtot = vtot + vrecv[i]
-    here = lax.broadcasted_iota(jnp.int32, (BR, BS), 0) == mine
-    row = jnp.sum(jnp.where(here, vtot, 0.0), axis=0, keepdims=True)
+        row = row + vrecv[i]
     vec_ref[...] = jnp.where(tile % 2 == 0, row[:, :ROWS], row[:, ROWS:])
 
     def collect_diagonal(i, carry):
@@ -471,10 +505,12 @@
 
     for u in range(2):
         for d in range(6):
-            g_copy(d, u).wait_send()
+            for t in range(3):
+                g_copy(d, u, t).wait_send()
             a_copy(d, u).wait_send()
     for h in range(2):
-        g_sib(h).wait_send()
+        for t in range(3):
+            g_sib(h, t).wait_send()
         a_sib(h).wait_send()
 
     def finish(i, carry):
@@ -521,24 +557,26 @@
         scratch_shapes=[
             pltpu.SMEM((1, N_REGION * CAP), jnp.int32),
             pltpu.VMEM((BR, N_REGION * CAP), jnp.int32),
-            pltpu.VMEM((14, HALF, HITS, BS), BF16),
-            pltpu.VMEM((CHUNKS, HALF, HITS, BS), BF16),
-            pltpu.VMEM((14, HALF, 256), BF16),
-            pltpu.VMEM((CHUNKS, HALF, 256), BF16),
+            pltpu.VMEM((14, 3, GROUP, HITS, BS), BF16),
+            pltpu.VMEM((CHUNKS, 3, GROUP, HITS, BS), BF16),
+            pltpu.VMEM((14, 3, GROUP, 256), BF16),
+            pltpu.VMEM((CHUNKS, 3, GROUP, 256), BF16),
             pltpu.VMEM((TRK, 256), BF16),
             pltpu.VMEM((WIDTH, HALF * HITS), BF16),
             pltpu.VMEM((CHUNKS, BR, HALF * HITS), BF16),
-            pltpu.VMEM((CHUNKS * 128, WIDTH + WIDTH // 2), BF16),
+            pltpu.VMEM((CHUNKS * 120, WIDTH + WIDTH // 2), BF16),
+            pltpu.VMEM((4, 256, 768), F32),
             pltpu.VMEM((WIDTH, BS), F32),
             pltpu.VMEM((BR, BS), F32),
+            pltpu.VMEM((BR, 1, BS), F32),
             pltpu.VMEM((16, 4, ROWS, BS), BF16),
             pltpu.VMEM((16, 4, ROWS, BS), BF16),
-            pltpu.VMEM((16, BR, BS), F32),
+            pltpu.VMEM((16, 1, BS), F32),
             pltpu.VMEM((16, ROWS, BS), BF16),
             pltpu.VMEM((16, ROWS, BS), BF16),
-            pltpu.VMEM((8, 32, BS), F32),
-            pltpu.VMEM((8, 32, BS), F32),
-            dma((14,)), dma((16,)), dma((14,)), dma((16,)),
+            pltpu.VMEM((8, 32, BS), BF16),
+            pltpu.VMEM((8, 32, BS), BF16),
+            dma((14, 3)), dma((16, 3)), dma((14,)), dma((16,)),
             dma((16,)), dma((16,)), dma((16,)), dma((16,)), dma((16,)), dma((16,)), dma((8,)), dma((8,)), dma,
         ],
         compiler_params=pltpu.CompilerParams(

time: 53.4 us -> 51.2 us (0.959)
  Pallas kernels: 49.6 us -> 47.6 us
    pallas_call x1, Pallas kernels: 49.6 us -> 47.6 us  [local(): pl.pallas_call(kernel, name='assemble', out_shape=(jax.ShapeDtypeStruct((...]
where the time goes in v4:
time: 51.2 us; the launch traced here: 51 us
  Pallas kernels  47.6 us (93%)
  local copies, waits for them, and re-layouts  2.8 us (5%)
  between operations  0.64 us (1%)
    pallas_call x1, Pallas kernels, local(): pl.pallas_call(kernel, name='assemble', out_shape=(jax.ShapeDtypeStruct((...  47.6 us
    unnamed x2, local copies, waits for them, and re-layouts  2.8 us

profile of v4, /device:TPU:8, one launch (start us, length us, event | category | flops | bytes accessed | tf_op | source)
XLA Modules:
  0.0 51.0 jit_solution(9622281988414623757)
XLA Ops:
  0.6 47.6 %assemble.1 = (f32[1,64,1024]{2,1,0:T(8,128)}, f32[1,64]{1,0:T(1,128)}) custom-call(s32[8]{0:T(128)} %place_ref.1, bf16[192,32,128]{2,1,0:T(8,128)(2,1)} %g_ref.1, bf16[5,32,192]{2,1,0:T(8,128)(2,1)} %bitcast.6, bf16[32,192]{1,0:T(8,128)(2,1)} %bitcast.8, bf16[32,192]{1,0:T(8,128)(2,1)} %bitcast.9, s32[32,192]{1,0:T(8,128)} %bitcast.7, s32[1,192]{1,0:T(1,128)} %bitcast.10, ...), custom_call_target="tpu_custom_call" | custom-call | tf_op jit(solution)/shard_map/assemble/pallas_call | solution.py:548
  48.2 1.7 %copy.12 = f32[1,64,1024]{2,1,0:T(8,128)} copy(f32[1,64,1024]{2,1,0:T(8,128)} %get-tuple-element.4) | data formatting | bytes 524288
  49.9 1.1 %copy.13 = f32[1,64]{1,0:T(1,128)} copy(f32[1,64]{1,0:T(1,128)} %get-tuple-element.5) | data formatting | bytes 512

commit v5 on v4

--- a/solution.py
+++ b/solution.py
@@ -70,7 +70,7 @@
     out_ref, vec_ref, idx_ref, idx_vec,
     gsend, grecv, asend, arecv, fitted, lhs, wp_buf, s_buf, p_acc, d_acc, v_acc, vsend,
     psend, precv, vrecv, dsend, drecv, xsend, xrecv,
-    gs_sem, gr_sem, as_sem, ar_sem, ps_sem, pr_sem, vs_sem, vr_sem, ds_sem, dr_sem, xs_sem, xr_sem, idx_sem,
+    gs_sem, gr_sem, as_sem, ar_sem, ps_sem, pr_sem, vs_sem, vr_sem, ds_sem, dr_sem, xs_sem, xr_sem, idx_sem, plane_sem, all_sem,
 ):
     region = lax.axis_index("region")
     tile = lax.axis_index("tile")
@@ -93,32 +93,22 @@
             pl.semaphore_signal(barrier, inc=1, device_id=neighbour(d, c))
     pl.semaphore_signal(barrier, inc=1, device_id=sibling)
 
-    def worker_of(i, rz):
-        wy, wx = i // 4, i % 4
-        return {"region": ((rz - wx - 2 * wy + 12) % 4) * 2 + core, "tile": i}
+    def along(axis, k):
+        steps = [k if axis == n else 0 for n in range(3)]
+        return device((x + steps[0]) % 4, (y + steps[1]) % 4, (z + steps[2]) % 4, core)
+
+    for axis in range(3):
+        pl.semaphore_signal(barrier, inc=1, device_id=along(axis, 2))
 
     own_worker = (x + 2 * y) % 4 == 0
-
-    def greet(i, carry):
-        @pl.when(jnp.logical_not(jnp.logical_and(own_worker, i == tile)))
-        def _():
-            pl.semaphore_signal(barrier, inc=1, device_id=worker_of(i, z))
-        return carry
-
-    lax.fori_loop(0, 16, greet, 0)
     mine = tile // 2
 
     def owner(a, e):
         return {"region": region, "tile": ((a + 8) % 8) * 2 + e}
 
-    for j in range(1, 4):
-        for e in range(2):
-            pl.semaphore_signal(barrier, inc=1, device_id=owner(mine - j, e))
-
-    @pl.when(mine >= 4)
-    def _():
-        for e in range(2):
-            pl.semaphore_signal(barrier, inc=1, device_id=owner(mine - 4, e))
+    def tell(sem, axis):
+        for k in range(1, 4):
+            pl.semaphore_signal(sem, inc=1, device_id=along(axis, k))
 
     reg = region_ref[...]
     tracks8 = lax.broadcasted_iota(jnp.int32, (BR, TRK), 0)
@@ -175,11 +165,11 @@
             for d in range(6):
                 gather(chunk_of(d, core ^ u), t, gsend, u * 6 + d)
                 if u == 0 and t == 0 and d == 0:
-                    pl.semaphore_wait(
-                        barrier, jnp.where(own_worker, 34, 35) + jnp.where(mine < 4, 2, 0))
+                    pl.semaphore_wait(barrier, 16)
                 g_copy(d, u, t).start()
 
     send_tracks(0)
+    tell(plane_sem, 1)
 
     live = lax.broadcasted_iota(jnp.int32, (HITS, TRK), 0) < count_ref[...]
     weight = jnp.where(live, weight_ref[...].astype(F32), 0.0)
@@ -205,6 +195,8 @@
         pick((colour * 2 + 1 - core) * 2 + h, asend, 12 + h)
         a_sib(h).start()
     send_tracks(1)
+    pl.semaphore_wait(plane_sem, 3)
+    tell(all_sem, 0)
     for h in range(2):
         for t in range(3):
             gather((colour * 2 + 1 - core) * 2 + h, t, gsend, 12 + h)
@@ -314,6 +306,7 @@
     lax.fori_loop(2, 5, batch, 0)
     accumulate(480, 720)
     lax.fori_loop(5, 8, batch, 0)
+    pl.semaphore_wait(all_sem, 3)
 
     def target(i):
         return {"region": colour * 2 + core, "tile": i}
@@ -533,6 +526,11 @@
     lax.fori_loop(0, 16, finish, 0)
 
 
+def hand_over(matrix_ref, vector_ref, out_ref, vec_ref):
+    out_ref[...] = matrix_ref[...]
+    vec_ref[...] = vector_ref[...]
+
+
 def local(
     global_deriv,
     local_deriv,
@@ -545,7 +543,7 @@
 ):
     vmem = pl.BlockSpec(memory_space=pltpu.VMEM)
     dma = pltpu.SemaphoreType.DMA
-    return pl.pallas_call(
+    matrix, vector = pl.pallas_call(
         kernel,
         name="assemble",
         out_shape=(
@@ -578,12 +576,23 @@
             pltpu.VMEM((8, 32, BS), BF16),
             dma((14, 3)), dma((16, 3)), dma((14,)), dma((16,)),
             dma((16,)), dma((16,)), dma((16,)), dma((16,)), dma((16,)), dma((16,)), dma((8,)), dma((8,)), dma,
+            pltpu.SemaphoreType.REGULAR, pltpu.SemaphoreType.REGULAR,
         ],
         compiler_params=pltpu.CompilerParams(
             collective_id=0, has_side_effects=True, vmem_limit_bytes=56 << 20),
     )(
         block_place, global_deriv, local_deriv.transpose(1, 2, 0), hit_weight.T, hit_resid.T,
         block_ids.T, hit_count.reshape(1, TRK), track_region.reshape(1, TRK))
+    return pl.pallas_call(
+        hand_over,
+        name="hand_over",
+        out_shape=(
+            jax.ShapeDtypeStruct((1, ROWS, WIDTH), F32),
+            jax.ShapeDtypeStruct((1, ROWS), F32),
+        ),
+        in_specs=[vmem, vmem],
+        out_specs=(vmem, vmem),
+    )(matrix, vector)
 
 
 def solution(mesh):

time: 51.2 us -> 48.1 us (0.939)
  local copies, waits for them, and re-layouts: 2.8 us -> 0 us
    unnamed x2 -> x0, local copies, waits for them, and re-layouts: 2.8 us -> none
    pallas_call x1, Pallas kernels: 47.6 us -> 45.6 us  [local(): pl.pallas_call(kernel, name='assemble', out_shape=(jax.ShapeDtypeStruct((...]
    pallas_call x0 -> x1, Pallas kernels: none -> 1.68 us  [local(): pl.pallas_call(hand_over, name='hand_over', out_shape=(jax.ShapeDtypeStru...]
where the time goes in v5:
time: 48.1 us; the launch traced here: 48 us
  Pallas kernels  47.3 us (98%)
  between operations  0.64 us (1%)
    pallas_call x1, Pallas kernels, local(): pl.pallas_call(kernel, name='assemble', out_shape=(jax.ShapeDtypeStruct((...  45.6 us
    pallas_call x1, Pallas kernels, local(): pl.pallas_call(hand_over, name='hand_over', out_shape=(jax.ShapeDtypeStru...  1.68 us

profile of v5, /device:TPU:8, one launch (start us, length us, event | category | flops | bytes accessed | tf_op | source)
XLA Modules:
  0.0 48.0 jit_solution(1656074767363786761)
XLA Ops:
  0.6 45.6 %assemble.1 = (f32[1,64,1024]{2,1,0:T(8,128)}, f32[1,64]{1,0:T(1,128)}) custom-call(s32[8]{0:T(128)} %place_ref.1, bf16[192,32,128]{2,1,0:T(8,128)(2,1)} %g_ref.1, bf16[5,32,192]{2,1,0:T(8,128)(2,1)} %bitcast.6, bf16[32,192]{1,0:T(8,128)(2,1)} %bitcast.8, bf16[32,192]{1,0:T(8,128)(2,1)} %bitcast.9, s32[32,192]{1,0:T(8,128)} %bitcast.7, s32[1,192]{1,0:T(1,128)} %bitcast.10, ...), custom_call_target="tpu_custom_call" | custom-call | tf_op jit(solution)/shard_map/assemble/pallas_call | solution.py:546
  46.3 1.7 %hand_over.1 = (f32[1,64,1024]{2,1,0:T(8,128)}, f32[1,64]{1,0:T(1,128)}) custom-call(f32[1,64,1024]{2,1,0:T(8,128)} %get-tuple-element.4.matrix_ref, f32[1,64]{1,0:T(1,128)} %get-tuple-element.5.vector_ref), custom_call_target="tpu_custom_call" | custom-call | tf_op jit(solution)/shard_map/hand_over/pallas_call | solution.py:586

commit v6 on v5

--- a/solution.py
+++ b/solution.py
@@ -70,7 +70,7 @@
     out_ref, vec_ref, idx_ref, idx_vec,
     gsend, grecv, asend, arecv, fitted, lhs, wp_buf, s_buf, p_acc, d_acc, v_acc, vsend,
     psend, precv, vrecv, dsend, drecv, xsend, xrecv,
-    gs_sem, gr_sem, as_sem, ar_sem, ps_sem, pr_sem, vs_sem, vr_sem, ds_sem, dr_sem, xs_sem, xr_sem, idx_sem, plane_sem, all_sem,
+    gs_sem, gr_sem, as_sem, ar_sem, ps_sem, pr_sem, vs_sem, vr_sem, ds_sem, dr_sem, xs_sem, xr_sem, idx_sem, pair_sem, plane_sem, all_sem,
 ):
     region = lax.axis_index("region")
     tile = lax.axis_index("tile")
@@ -89,8 +89,7 @@
 
     barrier = pltpu.get_barrier_semaphore()
     for d in range(6):
-        for c in range(2):
-            pl.semaphore_signal(barrier, inc=1, device_id=neighbour(d, c))
+        pl.semaphore_signal(barrier, inc=1, device_id=neighbour(d, core))
     pl.semaphore_signal(barrier, inc=1, device_id=sibling)
 
     def along(axis, k):
@@ -165,10 +164,11 @@
             for d in range(6):
                 gather(chunk_of(d, core ^ u), t, gsend, u * 6 + d)
                 if u == 0 and t == 0 and d == 0:
-                    pl.semaphore_wait(barrier, 16)
+                    pl.semaphore_wait(barrier, 10)
                 g_copy(d, u, t).start()
 
     send_tracks(0)
+    pl.semaphore_signal(pair_sem, inc=1, device_id=sibling)
     tell(plane_sem, 1)
 
     live = lax.broadcasted_iota(jnp.int32, (HITS, TRK), 0) < count_ref[...]
@@ -188,6 +188,8 @@
             ref[k, t] = picked[GROUP * t : GROUP * t + GROUP].astype(BF16)
 
     for u in range(2):
+        if u == 1:
+            pl.semaphore_wait(pair_sem, 1)
         for d in range(6):
             pick(chunk_of(d, core ^ u), asend, u * 6 + d)
             a_copy(d, u).start()
@@ -576,7 +578,7 @@
             pltpu.VMEM((8, 32, BS), BF16),
             dma((14, 3)), dma((16, 3)), dma((14,)), dma((16,)),
             dma((16,)), dma((16,)), dma((16,)), dma((16,)), dma((16,)), dma((16,)), dma((8,)), dma((8,)), dma,
-            pltpu.SemaphoreType.REGULAR, pltpu.SemaphoreType.REGULAR,
+            pltpu.SemaphoreType.REGULAR, pltpu.SemaphoreType.REGULAR, pltpu.SemaphoreType.REGULAR,
         ],
         compiler_params=pltpu.CompilerParams(
             collective_id=0, has_side_effects=True, vmem_limit_bytes=56 << 20),

time: 48.1 us -> 47 us (0.977)
  Pallas kernels: 47.3 us -> 46.2 us
    pallas_call x1, Pallas kernels: 45.6 us -> 44.5 us  [local(): pl.pallas_call(kernel, name='assemble', out_shape=(jax.ShapeDtypeStruct((...]
where the time goes in v6:
time: 47 us; the launch traced here: 46.8 us
  Pallas kernels  46.2 us (98%)
  between operations  0.64 us (1%)
    pallas_call x1, Pallas kernels, local(): pl.pallas_call(kernel, name='assemble', out_shape=(jax.ShapeDtypeStruct((...  44.5 us
    pallas_call x1, Pallas kernels, local(): pl.pallas_call(hand_over, name='hand_over', out_shape=(jax.ShapeDtypeStru...  1.68 us

profile of v6, /device:TPU:8, one launch (start us, length us, event | category | flops | bytes accessed | tf_op | source)
XLA Modules:
  0.0 46.8 jit_solution(13985711012359744076)
XLA Ops:
  0.6 44.5 %assemble.1 = (f32[1,64,1024]{2,1,0:T(8,128)}, f32[1,64]{1,0:T(1,128)}) custom-call(s32[8]{0:T(128)} %place_ref.1, bf16[192,32,128]{2,1,0:T(8,128)(2,1)} %g_ref.1, bf16[5,32,192]{2,1,0:T(8,128)(2,1)} %bitcast.6, bf16[32,192]{1,0:T(8,128)(2,1)} %bitcast.8, bf16[32,192]{1,0:T(8,128)(2,1)} %bitcast.9, s32[32,192]{1,0:T(8,128)} %bitcast.7, s32[1,192]{1,0:T(1,128)} %bitcast.10, ...), custom_call_target="tpu_custom_call" | custom-call | tf_op jit(solution)/shard_map/assemble/pallas_call | solution.py:548
  45.1 1.7 %hand_over.1 = (f32[1,64,1024]{2,1,0:T(8,128)}, f32[1,64]{1,0:T(1,128)}) custom-call(f32[1,64,1024]{2,1,0:T(8,128)} %get-tuple-element.4.matrix_ref, f32[1,64]{1,0:T(1,128)} %get-tuple-element.5.vector_ref), custom_call_target="tpu_custom_call" | custom-call | tf_op jit(solution)/shard_map/hand_over/pallas_call | solution.py:588

commit v7 on v6

--- a/solution.py
+++ b/solution.py
@@ -303,11 +303,19 @@
             return carry
         lax.fori_loop(0, 4, body, 0)
 
-    lax.fori_loop(0, 2, batch, 0)
-    accumulate(0, 480)
-    lax.fori_loop(2, 5, batch, 0)
-    accumulate(480, 720)
-    lax.fori_loop(5, 8, batch, 0)
+    def step(m, carry):
+        batch(m, carry)
+
+        @pl.when(m == 1)
+        def _():
+            accumulate(0, 480)
+
+        @pl.when(m == 4)
+        def _():
+            accumulate(480, 720)
+        return carry
+
+    lax.fori_loop(0, 8, step, 0)
     pl.semaphore_wait(all_sem, 3)
 
     def target(i):
@@ -398,6 +406,16 @@
 
     lax.fori_loop(0, 16, send_diagonal, 0)
 
+    for u in range(2):
+        for d in range(6):
+            for t in range(3):
+                g_copy(d, u, t).wait_send()
+            a_copy(d, u).wait_send()
+    for h in range(2):
+        for t in range(3):
+            g_sib(h, t).wait_send()
+        a_sib(h).wait_send()
+
     def p_arrival(i, count):
         return pltpu.make_async_remote_copy(
             src_ref=psend.at[0, pl.ds(0, count)], dst_ref=precv.at[i, pl.ds(0, count)],
@@ -468,6 +486,24 @@
         row = row + vrecv[i]
     vec_ref[...] = jnp.where(tile % 2 == 0, row[:, :ROWS], row[:, ROWS:])
 
+    def finish(i, carry):
+        other = jnp.logical_not(is_self(i))
+
+        @pl.when(jnp.logical_and(other, i < 8))
+        def _():
+            p_copy(i, 4).wait_send()
+
+        @pl.when(jnp.logical_and(other, i >= 8))
+        def _():
+            p_copy(i, 3).wait_send()
+
+        @pl.when(other)
+        def _():
+            v_copy(i).wait_send()
+        return carry
+
+    lax.fori_loop(0, 16, finish, 0)
+
     def collect_diagonal(i, carry):
         @pl.when(jnp.logical_not(is_self(i)))
         def _():
@@ -498,34 +534,13 @@
         for e in range(2):
             x_copy(4, e).wait_send()
 
-    for u in range(2):
-        for d in range(6):
-            for t in range(3):
-                g_copy(d, u, t).wait_send()
-            a_copy(d, u).wait_send()
-    for h in range(2):
-        for t in range(3):
-            g_sib(h, t).wait_send()
-        a_sib(h).wait_send()
-
-    def finish(i, carry):
-        other = jnp.logical_not(is_self(i))
-
-        @pl.when(jnp.logical_and(other, i < 8))
-        def _():
-            p_copy(i, 4).wait_send()
-
-        @pl.when(jnp.logical_and(other, i >= 8))
-        def _():
-            p_copy(i, 3).wait_send()
-
-        @pl.when(other)
-        def _():
-            v_copy(i).wait_send()
+    def finish_diagonal(i, carry):
+        @pl.when(jnp.logical_not(is_self(i)))
+        def _():
             d_copy(i).wait_send()
         return carry
 
-    lax.fori_loop(0, 16, finish, 0)
+    lax.fori_loop(0, 16, finish_diagonal, 0)
 
 
 def hand_over(matrix_ref, vector_ref, out_ref, vec_ref):

time: 47 us -> 46.9 us (level)
  no operation moved by 1% of the time
where the time goes in v7:
time: 46.9 us; the launch traced here: 46.7 us
  Pallas kernels  46.1 us (98%)
  between operations  0.64 us (1%)
    pallas_call x1, Pallas kernels, local(): pl.pallas_call(kernel, name='assemble', out_shape=(jax.ShapeDtypeStruct((...  44.4 us
    pallas_call x1, Pallas kernels, local(): pl.pallas_call(hand_over, name='hand_over', out_shape=(jax.ShapeDtypeStru...  1.68 us

profile of v7, /device:TPU:8, one launch (start us, length us, event | category | flops | bytes accessed | tf_op | source)
XLA Modules:
  0.0 46.7 jit_solution(1998672046193318187)
XLA Ops:
  0.6 44.4 %assemble.1 = (f32[1,64,1024]{2,1,0:T(8,128)}, f32[1,64]{1,0:T(1,128)}) custom-call(s32[8]{0:T(128)} %place_ref.1, bf16[192,32,128]{2,1,0:T(8,128)(2,1)} %g_ref.1, bf16[5,32,192]{2,1,0:T(8,128)(2,1)} %bitcast.6, bf16[32,192]{1,0:T(8,128)(2,1)} %bitcast.8, bf16[32,192]{1,0:T(8,128)(2,1)} %bitcast.9, s32[32,192]{1,0:T(8,128)} %bitcast.7, s32[1,192]{1,0:T(1,128)} %bitcast.10, ...), custom_call_target="tpu_custom_call" | custom-call | tf_op jit(solution)/shard_map/assemble/pallas_call | solution.py:563
  45.0 1.7 %hand_over.1 = (f32[1,64,1024]{2,1,0:T(8,128)}, f32[1,64]{1,0:T(1,128)}) custom-call(f32[1,64,1024]{2,1,0:T(8,128)} %get-tuple-element.4.matrix_ref, f32[1,64]{1,0:T(1,128)} %get-tuple-element.5.vector_ref), custom_call_target="tpu_custom_call" | custom-call | tf_op jit(solution)/shard_map/hand_over/pallas_call | solution.py:603

commit v8 on v7

--- a/solution.py
+++ b/solution.py
@@ -66,8 +66,8 @@
 
 
 def kernel(
-    place_ref, g_ref, slope_ref, weight_ref, resid_ref, block_ref, count_ref, region_ref,
-    out_ref, vec_ref, idx_ref, idx_vec,
+    place_ref, g_hbm, slope_ref, weight_ref, resid_ref, block_ref, count_ref, region_ref,
+    out_ref, vec_ref, g_ref, g_sem, idx_ref, idx_vec,
     gsend, grecv, asend, arecv, fitted, lhs, wp_buf, s_buf, p_acc, d_acc, v_acc, vsend,
     psend, precv, vrecv, dsend, drecv, xsend, xrecv,
     gs_sem, gr_sem, as_sem, ar_sem, ps_sem, pr_sem, vs_sem, vr_sem, ds_sem, dr_sem, xs_sem, xr_sem, idx_sem, pair_sem, plane_sem, all_sem,
@@ -86,6 +86,9 @@
         return device((x + dx + 4) % 4, (y + dy + 4) % 4, (z + dz + 4) % 4, ncore)
 
     sibling = device(x, y, z, 1 - core)
+
+    g_load = pltpu.make_async_copy(g_hbm, g_ref, g_sem)
+    g_load.start()
 
     barrier = pltpu.get_barrier_semaphore()
     for d in range(6):
@@ -123,6 +126,7 @@
     idx_vec[...] = jnp.dot(number, onehot, preferred_element_type=F32).astype(jnp.int32)
     idx_copy = pltpu.make_async_copy(idx_vec.at[pl.ds(0, 1)], idx_ref, idx_sem)
     idx_copy.start()
+    g_load.wait()
     idx_copy.wait()
 
     def gather(q, t, ref, k):
@@ -567,9 +571,11 @@
             jax.ShapeDtypeStruct((1, ROWS, WIDTH), F32),
             jax.ShapeDtypeStruct((1, ROWS), F32),
         ),
-        in_specs=[pl.BlockSpec(memory_space=pltpu.SMEM)] + [vmem] * 7,
+        in_specs=[pl.BlockSpec(memory_space=pltpu.SMEM), pl.BlockSpec(memory_space=pl.ANY)] + [vmem] * 6,
         out_specs=(vmem, vmem),
         scratch_shapes=[
+            pltpu.VMEM((TRK, HITS, BS), BF16),
+            dma,
             pltpu.SMEM((1, N_REGION * CAP), jnp.int32),
             pltpu.VMEM((BR, N_REGION * CAP), jnp.int32),
             pltpu.VMEM((14, 3, GROUP, HITS, BS), BF16),

time: 46.9 us -> 46.3 us (0.987)
  Pallas kernels: 46.1 us -> 45.5 us
    pallas_call x1, Pallas kernels: 44.4 us -> 43.8 us  [local(): pl.pallas_call(kernel, name='assemble', out_shape=(jax.ShapeDtypeStruct((...]
where the time goes in v8:
time: 46.3 us; the launch traced here: 46.2 us
  Pallas kernels  45.5 us (98%)
  between operations  0.64 us (1%)
    pallas_call x1, Pallas kernels, local(): pl.pallas_call(kernel, name='assemble', out_shape=(jax.ShapeDtypeStruct((...  43.8 us
    pallas_call x1, Pallas kernels, local(): pl.pallas_call(hand_over, name='hand_over', out_shape=(jax.ShapeDtypeStru...  1.68 us

profile of v8, /device:TPU:8, one launch (start us, length us, event | category | flops | bytes accessed | tf_op | source)
XLA Modules:
  0.0 46.2 jit_solution(15262826477156617906)
XLA Ops:
  0.6 43.8 %assemble.1 = (f32[1,64,1024]{2,1,0:T(8,128)}, f32[1,64]{1,0:T(1,128)}) custom-call(s32[8]{0:T(128)} %place_ref.1, bf16[192,32,128]{2,1,0:T(8,128)(2,1)} %g_hbm.1, bf16[5,32,192]{2,1,0:T(8,128)(2,1)} %bitcast.6, bf16[32,192]{1,0:T(8,128)(2,1)} %bitcast.8, bf16[32,192]{1,0:T(8,128)(2,1)} %bitcast.9, s32[32,192]{1,0:T(8,128)} %bitcast.7, s32[1,192]{1,0:T(1,128)} %bitcast.10, ...), custom_call_target="tpu_custom_call" | custom-call | tf_op jit(solution)/shard_map/assemble/pallas_call | solution.py:567
  44.5 1.7 %hand_over.1 = (f32[1,64,1024]{2,1,0:T(8,128)}, f32[1,64]{1,0:T(1,128)}) custom-call(f32[1,64,1024]{2,1,0:T(8,128)} %get-tuple-element.4.matrix_ref, f32[1,64]{1,0:T(1,128)} %get-tuple-element.5.vector_ref), custom_call_target="tpu_custom_call" | custom-call | tf_op jit(solution)/shard_map/hand_over/pallas_call | solution.py:609
